TPU v7x, 256 devices: a whole 4x4x8 slice. The times are simulated.
256 devices in a mesh: row: 32 (over z, y), col: 8 (over x, core).
Axes of the slice: x: 4, y: 4, z: 8, core: 2. Of those that a mesh axis runs over, the one named last changes fastest.
Arguments:
- anc_factor: float32 [32768, 8192], P('row', 'col'), may hold values from -0.046875 to 0.046875
- anc_solution: float32 [128, 49152], P('col', 'row'), may hold values from -6 to 6
- slot_row: int32 [32768], P('row'), may hold values from 0 to 1535, as said below
- tile_count: int32 [32], P('row'), may hold values from 2 to 8, as said below
- lower_factor: float32 [8, 1024, 8192], P(None, 'row', 'col'), may hold values from -0.109375 to 0.109375
- diag_inverse: float32 [8, 1024, 1024], P('col'), may hold values from -1.5 to 1.5, as said below
- rhs: float32 [128, 8192], P('row', 'col'), may hold values from -6 to 6
Outputs:
- solution: float32 [128, 8192], P('row', 'col')
Inputs may be any that keep to these rules, and one draw needn't show every extreme that they name: `slot_row`: within each aligned block of 1024 entries the values are distinct, and some block holds 1535. `tile_count`: some entry equals 8 in every draw. Each block diag_inverse[t] is lower triangular with a positive diagonal.
All inputs are finite; a program needn't handle non-finite values.
Results may differ from a plain program's by a relative error of at most 0.0001.
Values sent between devices are 32-bit elements; how exact they have to be, the bound alone decides.
No kernel may reach another device: no remote copies, remote signals or barrier semaphores. Data moves between devices by JAX's collectives and lax.ppermute only.
A program may use at most 64 MiB of HBM per device.

v0:
```python
import jax
import jax.numpy as jnp
from jax import lax
from jax.sharding import PartitionSpec as P

TILE = 128


def broadcast(array, axis, root):
    mine = lax.axis_index(axis) == root
    return lax.psum(jnp.where(mine, array, jnp.zeros_like(array)), axis)


def on_device(anc_factor, anc_solution, slot_row, tile_count, lower_factor, diag_inverse, rhs):
    highest = lax.Precision.HIGHEST
    column_index = lax.axis_index("col")
    panels = lower_factor.shape[0]
    rows_local = lower_factor.shape[1]
    slot_total = slot_row.shape[0]
    alive_mask = (jnp.arange(slot_total) < tile_count[0] * TILE).astype(jnp.float32)
    chosen = (
        jnp.take(lax.all_gather(anc_solution, "col", axis=0, tiled=True), slot_row, axis=1)
        * alive_mask[None, :]
    )
    ancestor_term = jnp.dot(
        chosen, anc_factor, precision=highest, preferred_element_type=jnp.float32
    )
    reduced = rhs - lax.psum_scatter(ancestor_term, "row", scatter_dimension=0, tiled=True)
    pending = jnp.zeros_like(reduced)
    result = jnp.zeros_like(reduced)
    panel_mask = (jnp.arange(panels) > column_index).astype(jnp.float32)
    lower_masked = lower_factor * panel_mask[:, None, None]
    lower_flat = lower_masked.reshape(panels * rows_local, lower_factor.shape[2])
    all_rhs = anc_solution.shape[0] * lax.axis_size("col")
    known_rows = jnp.zeros((all_rhs, panels * rows_local), jnp.float32)
    for target in range(panels - 1, -1, -1):
        if target < panels - 1:
            partial_sum = jnp.dot(
                known_rows, lower_flat, precision=highest, preferred_element_type=jnp.float32
            )
            pending = lax.psum_scatter(partial_sum, "row", scatter_dimension=0, tiled=True)
        solved = jnp.dot(
            reduced - pending,
            diag_inverse[0],
            precision=highest,
            preferred_element_type=jnp.float32,
        )
        result = jnp.where(column_index == target, solved, result)
        if target > 0:
            spread_rows = lax.all_to_all(solved, "row", split_axis=1, concat_axis=0, tiled=True)
            owner_rows = broadcast(spread_rows, "col", target)
            known_rows = known_rows.at[:, target * rows_local : (target + 1) * rows_local].set(
                owner_rows
            )
    return result


def solution(mesh):
    in_specs = (
        P("row", "col"),
        P("col", "row"),
        P("row"),
        P("row"),
        P(None, "row", "col"),
        P("col", None, None),
        P("row", "col"),
    )
    out_specs = P("row", "col")
    return jax.shard_map(
        on_device, mesh=mesh, in_specs=in_specs, out_specs=out_specs, check_vma=False
    )
```

profile of v0, /device:TPU:1, one launch (start us, length us, event | category | flops | bytes accessed | tf_op | source)
XLA Modules:
  0.0 1516.0 jit_solution(10085805310040251316)
XLA Ops:
  8.6 16.6 %all_gather.3 = f32[128,1536]{1,0:T(8,128)S(1)} all-gather(f32[16,1536]{1,0:T(8,128)} %param.22), channel_id=1, replica_groups=mesh['row'=32,'col'=8] {'col'}, dimensions={0}, use_global_device_ids=true | all-gather | bytes 884736 | tf_op jit(solution)/shard_map/all_gather | solution.py:22
  25.5 2.8 gather_fusion
  28.3 5.8 fusion.19
  35.4 143.7 %all-reduce.18.cloned.1.call-done = f32[128,1024]{1,0:T(8,128)} async-done(((f32[128,1024]{1,0:T(8,128)}), f32[128,1024]{1,0:T(8,128)}) %all-reduce.18.cloned.1.call-update) | async-done | bytes 524304
  179.1 0.8 dynamic-slice_subtract_fusion.14
  179.9 4.3 fusion.14
  185.0 5.1 all-to-all-start
  190.4 8.3 all-to-all-done
  199.3 0.7 reduce.50
  200.1 27.5 %psum.49 = f32[128,32]{1,0:T(8,128)S(1)} all-reduce(f32[128,32]{1,0:T(8,128)S(1)} %bitcast.107), channel_id=1, replica_groups=mesh['row'=32,'col'=8] {'col'}, use_global_device_ids=true, to_apply=%region_1.2 | all-reduce | flops 4096 | bytes 32768 | tf_op jit(solution)/shard_map/psum | solution.py:11
  227.6 1.5 fusion.25
  229.2 139.1 %all-reduce.20.cloned.1.call-done = f32[128,1024]{1,0:T(8,128)} async-done(((f32[128,1024]{1,0:T(8,128)}), f32[128,1024]{1,0:T(8,128)}) %all-reduce.20.cloned.1.call-update) | async-done | bytes 524304
  368.3 4.3 fusion.12
  373.4 5.1 all-to-all-start.1
  378.6 0.7 compare_reduce_fusion.5
  379.4 7.7 all-to-all-done.1
  387.1 0.7 reduce.51
  388.0 27.5 %psum.50 = f32[128,32]{1,0:T(8,128)S(1)} all-reduce(f32[128,32]{1,0:T(8,128)S(1)} %bitcast.108), channel_id=1, replica_groups=mesh['row'=32,'col'=8] {'col'}, use_global_device_ids=true, to_apply=%region_4.5 | all-reduce | flops 4096 | bytes 32768 | tf_op jit(solution)/shard_map/psum | solution.py:11
  416.8 1.5 fusion.38
  418.3 139.2 %all-reduce.22.cloned.1.call-done = f32[128,1024]{1,0:T(8,128)} async-done(((f32[128,1024]{1,0:T(8,128)}), f32[128,1024]{1,0:T(8,128)}) %all-reduce.22.cloned.1.call-update) | async-done | bytes 524304
  557.6 4.3 fusion.10
  562.7 5.1 all-to-all-start.2
  567.9 0.7 compare_reduce_fusion.4
  568.6 7.8 all-to-all-done.2
  576.4 0.7 reduce.52
  577.2 27.5 %psum.51 = f32[128,32]{1,0:T(8,128)S(1)} all-reduce(f32[128,32]{1,0:T(8,128)S(1)} %bitcast.109), channel_id=1, replica_groups=mesh['row'=32,'col'=8] {'col'}, use_global_device_ids=true, to_apply=%region_7.8 | all-reduce | flops 4096 | bytes 32768 | tf_op jit(solution)/shard_map/psum | solution.py:11
  604.7 0.8 slice_select_fusion.4
  606.1 1.5 fusion.39
  607.7 139.0 %all-reduce.24.cloned.1.call-done = f32[128,1024]{1,0:T(8,128)} async-done(((f32[128,1024]{1,0:T(8,128)}), f32[128,1024]{1,0:T(8,128)}) %all-reduce.24.cloned.1.call-update) | async-done | bytes 524304
  746.7 4.3 fusion.8
  751.8 5.1 all-to-all-start.3
  757.8 7.8 all-to-all-done.3
  765.5 0.7 reduce.53
  766.4 27.5 %psum.52 = f32[128,32]{1,0:T(8,128)S(1)} all-reduce(f32[128,32]{1,0:T(8,128)S(1)} %bitcast.110), channel_id=1, replica_groups=mesh['row'=32,'col'=8] {'col'}, use_global_device_ids=true, to_apply=%region_10.11 | all-reduce | flops 4096 | bytes 32768 | tf_op jit(solution)/shard_map/psum | solution.py:11
  795.0 1.5 fusion.40
  796.6 139.0 %all-reduce.26.cloned.1.call-done = f32[128,1024]{1,0:T(8,128)} async-done(((f32[128,1024]{1,0:T(8,128)}), f32[128,1024]{1,0:T(8,128)}) %all-reduce.26.cloned.1.call-update) | async-done | bytes 524304
  935.6 4.3 fusion.6
  940.7 5.4 all-to-all-start.4
  946.9 7.8 all-to-all-done.4
  954.6 0.7 reduce.54
  955.5 27.5 %psum.53 = f32[128,32]{1,0:T(8,128)S(1)} all-reduce(f32[128,32]{1,0:T(8,128)S(1)} %bitcast.111), channel_id=1, replica_groups=mesh['row'=32,'col'=8] {'col'}, use_global_device_ids=true, to_apply=%region_13.14 | all-reduce | flops 4096 | bytes 32768 | tf_op jit(solution)/shard_map/psum | solution.py:11
  983.0 0.8 slice_select_fusion.2
  983.8 0.8 scatter.30
  984.6 1.5 fusion.41
  986.2 139.0 %all-reduce.28.cloned.1.call-done = f32[128,1024]{1,0:T(8,128)} async-done(((f32[128,1024]{1,0:T(8,128)}), f32[128,1024]{1,0:T(8,128)}) %all-reduce.28.cloned.1.call-update) | async-done | bytes 524304
  1125.2 4.3 fusion.4
  1130.3 5.1 all-to-all-start.5
  1136.2 7.8 all-to-all-done.5
  1144.0 0.7 reduce.55
  1144.9 27.5 %psum.54 = f32[128,32]{1,0:T(8,128)S(1)} all-reduce(f32[128,32]{1,0:T(8,128)S(1)} %bitcast.112), channel_id=1, replica_groups=mesh['row'=32,'col'=8] {'col'}, use_global_device_ids=true, to_apply=%region_16.17 | all-reduce | flops 4096 | bytes 32768 | tf_op jit(solution)/shard_map/psum | solution.py:11
  1172.4 0.8 slice_select_fusion.1
  1173.1 0.8 scatter.31
  1174.0 1.5 fusion.42
  1175.5 139.1 %all-reduce.30.cloned.1.call-done = f32[128,1024]{1,0:T(8,128)} async-done(((f32[128,1024]{1,0:T(8,128)}), f32[128,1024]{1,0:T(8,128)}) %all-reduce.30.cloned.1.call-update) | async-done | bytes 524304
  1314.6 4.3 fusion.2
  1319.8 5.1 all-to-all-start.6
  1325.7 7.8 all-to-all-done.6
  1333.4 0.7 reduce.56
  1334.3 27.5 %psum.55 = f32[128,32]{1,0:T(8,128)S(1)} all-reduce(f32[128,32]{1,0:T(8,128)S(1)} %bitcast.113), channel_id=1, replica_groups=mesh['row'=32,'col'=8] {'col'}, use_global_device_ids=true, to_apply=%region_19.20 | all-reduce | flops 4096 | bytes 32768 | tf_op jit(solution)/shard_map/psum | solution.py:11
  1361.8 0.8 slice_select_fusion
  1362.6 0.8 scatter.34
  1363.4 1.5 fusion.43
  1365.0 139.3 %all-reduce.32.cloned.1.call-done = f32[128,1024]{1,0:T(8,128)} async-done(((f32[128,1024]{1,0:T(8,128)}), f32[128,1024]{1,0:T(8,128)}) %all-reduce.32.cloned.1.call-update) | async-done | bytes 524304
  1504.3 4.9 fusion.16
  (74 shorter events, 16.1 us)
Async XLA Ops:
  6.5 172.6 %all-reduce.18.cloned.1.call-start = ((), (), s32[]{:S(2)}) async-start(), calls=%async_computation.7 | async-start | bytes 1048576
  25.5 8.7 copy-start.2
  25.5 153.6 %copy-start.1 = (f32[4,1024]{1,0:T(4,128)S(1)}, f32[4,1024]{1,0:T(4,128)}, u32[]{:S(2)}) copy-start(f32[4,1024]{1,0:T(4,128)} %param.27) | copy-start | bytes 49156
  28.3 161.9 %copy-start = (f32[8,32,1024]{2,1,0:T(8,128)S(1)}, f32[8,32,1024]{2,1,0:T(8,128)}, u32[]{:S(2)}) copy-start(f32[8,32,1024]{2,1,0:T(8,128)} %param.25) | copy-start | bytes 3145732
  185.0 13.7 all-to-all-start
  190.1 178.2 %all-reduce.20.cloned.1.call-start = ((), (), s32[]{:S(2)}) async-start(), calls=%async_computation.8 | async-start | bytes 1048576
  373.4 13.7 all-to-all-start.1
  378.6 179.0 %all-reduce.22.cloned.1.call-start = ((), (), s32[]{:S(2)}) async-start(), calls=%async_computation.9 | async-start | bytes 1048576
  562.7 13.7 all-to-all-start.2
  567.8 178.9 %all-reduce.24.cloned.1.call-start = ((), (), s32[]{:S(2)}) async-start(), calls=%async_computation.10 | async-start | bytes 1048576
  751.8 13.7 all-to-all-start.3
  757.0 178.6 %all-reduce.26.cloned.1.call-start = ((), (), s32[]{:S(2)}) async-start(), calls=%async_computation.11 | async-start | bytes 1048576
  940.7 13.9 all-to-all-start.4
  946.1 179.1 %all-reduce.28.cloned.1.call-start = ((), (), s32[]{:S(2)}) async-start(), calls=%async_computation.12 | async-start | bytes 1048576
  1130.3 13.7 all-to-all-start.5
  1135.5 179.2 %all-reduce.30.cloned.1.call-start = ((), (), s32[]{:S(2)}) async-start(), calls=%async_computation.13 | async-start | bytes 1048576
  1319.8 13.7 all-to-all-start.6
  1324.9 179.4 %all-reduce.32.cloned.1.call-start = ((), (), s32[]{:S(2)}) async-start(), calls=%async_computation.14 | async-start | bytes 1048576
Sparse Core Ops, SparseCore 0:
  34.3 144.7 all-reduce.17
  229.3 138.9 all-reduce.19
  418.5 139.0 all-reduce.21
  607.8 138.8 all-reduce.23
  796.7 138.8 all-reduce.25
  986.3 138.8 all-reduce.27
  1175.7 138.9 all-reduce.29
  1365.1 139.1 all-reduce.31
where the time goes:
time: 1520 us
  waiting for transfers between devices  1170 us (77%)
  blocking collectives  209 us (14%)
  matrix products  51.4 us (3%)
  starting transfers between devices  36.5 us (2%)
  other arithmetic  16.3 us (1%)
  between operations  15.3 us (1%)
    unnamed x16, waiting for transfers between devices  1120 us
    psum x7, blocking collectives, broadcast(): return lax.psum(jnp.where(mine, array, jnp.zeros_like(array)), axis)  193 us
    all_to_all x7, waiting for transfers between devices, on_device(): lax.all_to_all(solved, 'row', split_axis=1, concat_axis=0, tiled=True)  54.8 us
    all_to_all x7, starting transfers between devices, on_device(): lax.all_to_all(solved, 'row', split_axis=1, concat_axis=0, tiled=True)  36.2 us
    dot_general x8, matrix products, on_device(): jnp.dot(reduced - pending, diag_inverse[0], precision=highest, preferred_...  34.9 us
  transfers between devices with their start and end apart: 15, of which 15 were waited for; matrix products, arithmetic and copies ran while one was open for 0% of the time, Pallas kernels for 0%

commit v1 on v0

v1 whole, which is shorter than its diff:
```python
import jax
import jax.numpy as jnp
from jax import lax
from jax.sharding import PartitionSpec as P

TILE = 128
HALF = 4


def dot(a, b, precision=lax.Precision.HIGHEST):
    return jnp.dot(a, b, precision=precision, preferred_element_type=jnp.float32)


def scatter_rows(partial_sum):
    rows = lax.axis_size("row")
    parts = partial_sum.reshape(rows, -1, partial_sum.shape[1])
    return lax.all_to_all(parts, "row", 0, 0).sum(axis=0)


def on_device(anc_factor, anc_solution, slot_row, tile_count, lower_factor, diag_inverse, rhs):
    column = lax.axis_index("col")
    panels, rows_local, width = lower_factor.shape
    base = column // HALF * HALF
    place = column % HALF
    diag = diag_inverse[0]

    scaled = dot(lower_factor.reshape(panels * rows_local, width), diag)
    scaled = scaled.reshape(panels, rows_local, width)

    def block(k):
        return lax.dynamic_index_in_dim(scaled, k, 0, keepdims=False)

    own = block(base + jnp.where(place == 0, 3, 2))
    lent = lax.ppermute(
        block(base + jnp.where(place == 0, 2, 3)), "col", [(0, 2), (1, 3), (4, 6), (5, 7)]
    )
    between = jnp.where(place < 2, own, lent)
    within = block(jnp.minimum(column + 1, panels - 1))
    near = lax.all_gather(
        jnp.concatenate([between, within], axis=1), "row", axis=0, tiled=True
    )

    alive = jnp.arange(slot_row.shape[0]) < tile_count[0] * TILE
    mine = jnp.where(alive[None, :], jnp.take(anc_solution, slot_row, axis=1), 0.0)
    chosen = lax.all_gather(mine, "col", axis=0, tiled=True)
    updated = rhs - scatter_rows(dot(chosen, anc_factor))
    value = dot(updated, diag)

    between_full = near[:, :width]
    within_full = near[:, width:]

    def inside_pair(value, source):
        got = lax.ppermute(value, "col", [(source, source - 1)])
        return value - dot(got, within_full, lax.Precision.HIGH)

    def solve_half(value, low):
        a, b, c, d = low, low + 1, low + 2, low + 3
        value = inside_pair(value, d)
        got = lax.ppermute(value, "col", [(d, a), (c, b)])
        upper = (column == c) | (column == d)
        term = dot(jnp.where(upper, value, got), between_full, lax.Precision.HIGH)
        back = lax.ppermute(term, "col", [(d, b), (c, a)])
        lower = (column == a) | (column == b)
        value = value - jnp.where(lower, term + back, 0.0)
        return inside_pair(value, b)

    value = solve_half(value, HALF)

    spread = lax.all_to_all(value, "row", split_axis=1, concat_axis=0, tiled=True)
    known, weights = [], []
    for shift in range(HALF):
        pairs = [(HALF + (i + shift) % HALF, i) for i in range(HALF)]
        known.append(lax.ppermute(spread, "col", pairs))
        weights.append(block(HALF + (place + shift) % HALF))
    term = dot(jnp.concatenate(known, axis=1), jnp.concatenate(weights, axis=0))
    value = value - scatter_rows(term)

    return solve_half(value, 0)


def solution(mesh):
    in_specs = (
        P("row", "col"),
        P("col", "row"),
        P("row"),
        P("row"),
        P(None, "row", "col"),
        P("col", None, None),
        P("row", "col"),
    )
    out_specs = P("row", "col")
    return jax.shard_map(
        on_device, mesh=mesh, in_specs=in_specs, out_specs=out_specs, check_vma=False
    )
```

time: 1520 us -> 231 us (0.15)
  waiting for transfers between devices: 1170 us -> 78.8 us
  blocking collectives: 209 us -> 75 us
  starting transfers between devices: 36.5 us -> 18.6 us
  matrix products: 51.4 us -> 35.7 us
    unnamed x16 -> x1, waiting for transfers between devices: 1120 us -> 0.02 us
    psum x7 -> x0, blocking collectives: 193 us -> none  [broadcast(): return lax.psum(jnp.where(mine, array, jnp.zeros_like(array)), axis)]
    all_to_all x0 -> x3, blocking collectives: none -> 59.8 us  [the longest x2 46 us: scatter_rows(): return lax.all_to_all(parts, 'row', 0, 0).sum(axis=0)]
    all_to_all x7 -> x0, waiting for transfers between devices: 54.8 us -> none  [on_device(): lax.all_to_all(solved, 'row', split_axis=1, concat_axis=0, tiled=True)]
    all_gather x0 -> x1, waiting for transfers between devices: none -> 47.5 us  [on_device(): lax.all_gather(jnp.concatenate([between, within], axis=1), 'row', axis=0,...]
    all_to_all x7 -> x0, starting transfers between devices: 36.2 us -> none  [on_device(): lax.all_to_all(solved, 'row', split_axis=1, concat_axis=0, tiled=True)]
    ppermute x0 -> x13, waiting for transfers between devices: none -> 31.3 us  [the longest x4 16.9 us: on_device(): known.append(lax.ppermute(spread, 'col', pairs))]
    ppermute x0 -> x13, starting transfers between devices: none -> 18.6 us  [the longest x4 5.6 us: inside_pair(): got = lax.ppermute(value, 'col', [(source, source - 1)])]
  transfers between devices with their start and end apart: 15 -> 14, of which waited for: 15 -> 7; matrix products, arithmetic and copies ran while one was open for 0% -> 6% of each run, Pallas kernels for 0% -> 0%
where the time goes in v1:
time: 231 us; the launch traced here: 230 us
  waiting for transfers between devices  78.8 us (34%)
  blocking collectives  75 us (32%)
  matrix products  35.7 us (15%)
  starting transfers between devices  18.6 us (8%)
  between operations  14.4 us (6%)
  local copies, waits for them, and re-layouts  5.7 us (2%)
    all_gather x1, waiting for transfers between devices, on_device(): lax.all_gather(jnp.concatenate([between, within], axis=1), 'row', axis=0,...  47.5 us
    all_to_all x2, blocking collectives, scatter_rows(): return lax.all_to_all(parts, 'row', 0, 0).sum(axis=0)  46 us
    dot_general x10, matrix products, dot(): jnp.dot(a, b, precision=precision, preferred_element_type=jnp.float32)  35.7 us
    ppermute x4, waiting for transfers between devices, on_device(): known.append(lax.ppermute(spread, 'col', pairs))  16.9 us
    all_gather x1, blocking collectives, on_device(): chosen = lax.all_gather(mine, 'col', axis=0, tiled=True)  15.3 us
    all_to_all x1, blocking collectives, on_device(): lax.all_to_all(value, 'row', split_axis=1, concat_axis=0, tiled=True)  13.8 us
    ppermute x2, waiting for transfers between devices, solve_half(): got = lax.ppermute(value, 'col', [(d, a), (c, b)])  8.28 us
    ppermute x4, starting transfers between devices, inside_pair(): got = lax.ppermute(value, 'col', [(source, source - 1)])  5.6 us
  transfers between devices with their start and end apart: 14, of which 7 were waited for; matrix products, arithmetic and copies ran while one was open for 6% of the time, Pallas kernels for 0%

profile of v1, /device:TPU:1, one launch (start us, length us, event | category | flops | bytes accessed | tf_op | source)
XLA Modules:
  0.0 230.3 jit_solution(15150785125083024454)
XLA Ops:
  6.5 0.0 copy-start
  6.5 0.0 all-gather.2.cloned.1.call-start
  6.5 1.2 copy-done
  7.8 0.0 copy-start.1
  7.8 5.7 %fusion = f32[8,32,1024]{2,1,0:T(8,128)S(1)} fusion(f32[8,32,1024]{2,1,0:T(8,128)S(1)} %copy-done, f32[1,1024,1024]{2,1,0:T(8,128)} %param.12), kind=kOutput, calls=%fused_computation.1 | convolution fusion | flops 3221225472 | bytes 6291456 | tf_op jit(solution)/shard_map/dot_general | solution.py:11
  13.5 0.1 dynamic-slice_bitcast_fusion.3
  13.6 3.9 %collective-permute-start.1 = (f32[32,1024]{1,0:T(8,128)S(1)}, f32[32,1024]{1,0:T(8,128)S(1)}, u32[]{:S(2)}, u32[]{:S(2)}) collective-permute-start(f32[32,1024]{1,0:T(8,128)S(1)} %get-tuple-element.10), channel_id=1, source_target_pairs={{0,2},{1,3},{4,6},{5,7},{8,10},{9,11},{12,14},{13,15},{16,18},{17,... | collective-permute-start | bytes 393224 | tf_op jit(solution)/shard_map/ppermute | solution.py:34
  17.6 2.1 collective-permute-done.1
  19.7 0.7 pad_maximum_fusion
  20.5 0.0 all-gather.2.cloned.1.call-update
  20.5 0.0 copy-done.1
  20.5 0.3 copy.11
  21.4 0.0 copy-done.3
  21.5 2.8 %gather_fusion = f32[1024,16]{1,0:T(8,128)S(1)} fusion(f32[16,1536]{0,1:T(8,128)S(1)} %copy.11, s32[1024]{0:T(1024)S(1)} %fusion.48), kind=kCustom, calls=%fused_computation | custom fusion | bytes 135168 | tf_op jit(solution)/shard_map/jit(_take)/gather | solution.py:44
  24.3 0.3 select_bitcast_fusion
  24.6 0.2 copy.12
  24.8 15.3 %all_gather.6 = f32[128,1024]{1,0:T(8,128)S(1)} all-gather(f32[16,1024]{1,0:T(8,128)S(1)} %copy.12), channel_id=1, replica_groups=mesh['row'=32,'col'=8] {'col'}, dimensions={0}, use_global_device_ids=true | all-gather | bytes 589824 | tf_op jit(solution)/shard_map/all_gather | solution.py:45
  40.1 4.6 %fusion.50 = f32[128,1024]{1,0:T(8,128)S(1)} fusion(f32[128,1024]{1,0:T(8,128)S(1)} %all_gather.6, f32[1024,1024]{1,0:T(8,128)} %param.7), kind=kOutput, calls=%fused_computation.58 | convolution fusion | flops 1610612736 | bytes 5242880 | tf_op jit(solution)/shard_map/dot_general | solution.py:11
  44.7 0.1 reshape.24
  44.8 28.8 %all_to_all.29 = f32[32,4,1024]{2,1,0:T(4,128)S(1)} all-to-all(f32[32,4,1024]{2,1,0:T(4,128)S(1)} %reshape.24), channel_id=1, replica_groups=mesh['row'=32,'col'=8] {'row'}, dimensions={0} | all-to-all | bytes 1048576 | tf_op jit(solution)/shard_map/all_to_all | solution.py:17
  73.6 0.1 reduce_sum.18
  73.7 0.0 copy-done.2
  73.7 4.3 %fusion.2 = f32[4,1024]{1,0:T(4,128)S(1)} fusion(f32[1,1024,1024]{2,1,0:T(8,128)} %param.12, f32[4,1024]{1,0:T(4,128)S(1)} %copy-done.2, f32[4,1024]{1,0:T(4,128)S(1)} %reduce_sum.18), kind=kOutput, calls=%fused_computation.3 | convolution fusion | flops 50335744 | bytes 4243456 | tf_op jit(solution)/shard_map/dot_general | solution.py:11
  78.0 0.7 collective-permute-start
  78.6 0.0 collective-permute-done
  78.7 47.5 %all-gather.2.cloned.1.call-done = f32[1024,2048]{1,0:T(8,128)} async-done(((f32[32,2048]{1,0:T(8,128)}), f32[1024,2048]{1,0:T(8,128)}) %all-gather.2.cloned.1.call-update) | async-done | bytes 8388624 | tf_op jit(solution)/shard_map/all_gather | solution.py:39
  126.2 3.3 %fusion.16 = f32[4,1024]{1,0:T(4,128)S(1)} fusion(f32[4,1024]{1,0:T(4,128)S(1)} %fusion.2, f32[4,1024]{1,0:T(4,128)S(1)} %collective-permute-done, f32[1024,2048]{1,0:T(8,128)} %all-gather.2.cloned.1.call-done), kind=kOutput, calls=%fused_computation.17 | convolution fusion | flops 25169920 | bytes 4243456 | tf_op jit(solution)/shard_map/dot_general | solution.py:11
  129.5 0.7 collective-permute-start.2
  130.1 0.0 collective-permute-done.2
  130.1 3.3 %fusion.6 = f32[4,1024]{1,0:T(4,128)S(1)} fusion(f32[1024,2048]{1,0:T(8,128)} %all-gather.2.cloned.1.call-done, f32[4,1024]{1,0:T(4,128)S(1)} %fusion.16, f32[4,1024]{1,0:T(4,128)S(1)} %collective-permute-done.2, pred[]{:T(512)S(6)} %or.13), kind=kOutput, calls=%fused_computation.7 | convolution fusion | flops 25169920 | bytes 4243457 | tf_op jit(solution)/shard_map/dot_general | solution.py:11
  133.5 0.7 collective-permute-start.3
  134.1 0.0 collective-permute-done.3
  134.2 0.8 collective-permute-start.4
  135.0 0.0 collective-permute-done.4
  135.0 3.3 %fusion.19 = f32[4,1024]{1,0:T(4,128)S(1)} fusion(f32[4,1024]{1,0:T(4,128)S(1)} %select_subtract_fusion.1, f32[4,1024]{1,0:T(4,128)S(1)} %collective-permute-done.4, f32[1024,2048]{1,0:T(8,128)} %all-gather.2.cloned.1.call-done), kind=kOutput, calls=%fused_computation.18 | convolution fusion | flops 25169920 | bytes 4243456 | tf_op jit(solution)/shard_map/dot_general | solution.py:11
  138.3 0.1 all_to_all.21
  138.5 0.1 reshape.36
  138.6 13.8 %all_to_all.30 = f32[32,1,128]{2,1,0:T(1,128)S(1)} all-to-all(f32[32,1,128]{2,1,0:T(1,128)S(1)} %reshape.36), channel_id=1, replica_groups=mesh['row'=32,'col'=8] {'row'}, dimensions={0} | all-to-all | bytes 32768 | tf_op jit(solution)/shard_map/all_to_all | solution.py:69
  152.4 0.5 broadcast.27
  152.9 0.7 reduce
  153.6 0.1 reshape.37
  153.7 1.3 collective-permute-start.8
  155.0 1.3 collective-permute-start.7
  156.3 1.3 collective-permute-start.6
  157.6 1.3 collective-permute-start.5
  158.9 15.3 %collective-permute-done.8 = f32[128,32]{1,0:T(8,128)S(1)} collective-permute-done((f32[128,32]{1,0:T(8,128)S(1)}, f32[128,32]{1,0:T(8,128)S(1)}, u32[]{:S(2)}, u32[]{:S(2)}) %collective-permute-start.8) | collective-permute-done | bytes 16416 | tf_op jit(solution)/shard_map/ppermute | solution.py:73
  174.2 0.0 collective-permute-done.7
  174.2 0.0 collective-permute-done.6
  174.2 1.6 collective-permute-done.5
  175.8 0.6 fusion.28
  176.4 0.1 reshape.25
  176.6 17.2 %all_to_all.31 = f32[32,4,1024]{2,1,0:T(4,128)S(1)} all-to-all(f32[32,4,1024]{2,1,0:T(4,128)S(1)} %reshape.25), channel_id=1, replica_groups=mesh['row'=32,'col'=8] {'row'}, dimensions={0} | all-to-all | bytes 1048576 | tf_op jit(solution)/shard_map/all_to_all | solution.py:17
  193.8 0.1 reduce_sum.19
  193.9 0.7 collective-permute-start.9
  194.6 0.0 collective-permute-done.9
  194.6 3.3 %fusion.22 = f32[4,1024]{1,0:T(4,128)S(1)} fusion(f32[4,1024]{1,0:T(4,128)S(1)} %sub.33, f32[4,1024]{1,0:T(4,128)S(1)} %collective-permute-done.9, f32[1024,2048]{1,0:T(8,128)} %all-gather.2.cloned.1.call-done), kind=kOutput, calls=%fused_computation.19 | convolution fusion | flops 25169920 | bytes 4243456 | tf_op jit(solution)/shard_map/dot_general | solution.py:11
  197.9 1.3 collective-permute-start.10
  199.2 8.3 %collective-permute-done.10 = f32[4,1024]{1,0:T(4,128)S(1)} collective-permute-done((f32[4,1024]{1,0:T(4,128)S(1)}, f32[4,1024]{1,0:T(4,128)S(1)}, u32[]{:S(2)}, u32[]{:S(2)}) %collective-permute-start.10) | collective-permute-done | bytes 16416 | tf_op jit(solution)/shard_map/ppermute | solution.py:59
  207.5 3.3 %fusion.4 = f32[4,1024]{1,0:T(4,128)S(1)} fusion(f32[1024,2048]{1,0:T(8,128)} %all-gather.2.cloned.1.call-done, f32[4,1024]{1,0:T(4,128)S(1)} %fusion.22, f32[4,1024]{1,0:T(4,128)S(1)} %collective-permute-done.10, pred[]{:T(512)S(6)} %or.15), kind=kOutput, calls=%fused_computation.5 | convolution fusion | flops 25169920 | bytes 4243457 | tf_op jit(solution)/shard_map/dot_general | solution.py:11
  210.8 1.3 collective-permute-start.11
  212.1 3.2 %collective-permute-done.11 = f32[4,1024]{1,0:T(4,128)S(1)} collective-permute-done((f32[4,1024]{1,0:T(4,128)S(1)}, f32[4,1024]{1,0:T(4,128)S(1)}, u32[]{:S(2)}, u32[]{:S(2)}) %collective-permute-start.11) | collective-permute-done | bytes 16416 | tf_op jit(solution)/shard_map/ppermute | solution.py:62
  215.3 3.4 %collective-permute-start.12 = (f32[4,1024]{1,0:T(4,128)S(1)}, f32[4,1024]{1,0:T(4,128)S(1)}, u32[]{:S(2)}, u32[]{:S(2)}) collective-permute-start(f32[4,1024]{1,0:T(4,128)S(1)} %select_subtract_fusion), channel_id=1, source_target_pairs={{1,0},{9,8},{17,16},{25,24},{33,32},{41,40},{49,48},{57,56},{65,64... | collective-permute-start | bytes 49160 | tf_op jit(solution)/shard_map/ppermute | solution.py:53
  218.7 0.8 collective-permute-done.12
  219.6 3.9 %fusion.25 = f32[4,1024]{1,0:T(4,128)} fusion(f32[4,1024]{1,0:T(4,128)S(1)} %select_subtract_fusion, f32[4,1024]{1,0:T(4,128)S(1)} %collective-permute-done.12, f32[1024,2048]{1,0:T(8,128)} %all-gather.2.cloned.1.call-done), kind=kOutput, calls=%fused_computation.20 | convolution fusion | flops 25169920 | bytes 4243456 | tf_op jit(solution)/shard_map/dot_general | solution.py:11
  (9 shorter events, 0.1 us)
Async XLA Ops:
  6.5 1.2 copy-start
  6.5 119.6 %all-gather.2.cloned.1.call-start = ((), (), s32[]{:S(2)}) async-start(), calls=%async_computation.3 | async-start | bytes 8650752 | tf_op jit(solution)/shard_map/all_gather | solution.py:39
  7.8 12.7 %copy-start.1 = (f32[16,1536]{1,0:T(8,128)S(1)}, f32[16,1536]{1,0:T(8,128)}, u32[]{:S(2)}) copy-start(f32[16,1536]{1,0:T(8,128)} %param.8) | copy-start | bytes 294916
  7.8 13.7 %copy-start.3 = (s32[1024]{0:T(1024)S(1)}, s32[1024]{0:T(1024)}, u32[]{:S(2)}) copy-start(s32[1024]{0:T(1024)} %param.9) | copy-start | bytes 12292
  13.6 6.1 %collective-permute-start.1 = (f32[32,1024]{1,0:T(8,128)S(1)}, f32[32,1024]{1,0:T(8,128)S(1)}, u32[]{:S(2)}, u32[]{:S(2)}) collective-permute-start(f32[32,1024]{1,0:T(8,128)S(1)} %get-tuple-element.10), channel_id=1, source_target_pairs={{0,2},{1,3},{4,6},{5,7},{8,10},{9,11},{12,14},{13,15},{16,18},{17,... | collective-permute-start | bytes 393224 | tf_op jit(solution)/shard_map/ppermute | solution.py:34
  24.8 48.9 %copy-start.2 = (f32[4,1024]{1,0:T(4,128)S(1)}, f32[4,1024]{1,0:T(4,128)}, u32[]{:S(2)}) copy-start(f32[4,1024]{1,0:T(4,128)} %param.13) | copy-start | bytes 49156
  78.0 0.7 collective-permute-start
  129.5 0.7 collective-permute-start.2
  133.5 0.7 collective-permute-start.3
  134.2 0.9 collective-permute-start.4
  153.7 20.5 %collective-permute-start.8 = (f32[128,32]{1,0:T(8,128)S(1)}, f32[128,32]{1,0:T(8,128)S(1)}, u32[]{:S(2)}, u32[]{:S(2)}) collective-permute-start(f32[128,32]{1,0:T(8,128)S(1)} %bitcast.38), channel_id=1, source_target_pairs={{7,0},{4,1},{5,2},{6,3},{15,8},{12,9},{13,10},{14,11},{23,16},{20,... | collective-permute-start | bytes 49160 | tf_op jit(solution)/shard_map/ppermute | solution.py:73
  155.0 19.2 %collective-permute-start.7 = (f32[128,32]{1,0:T(8,128)S(1)}, f32[128,32]{1,0:T(8,128)S(1)}, u32[]{:S(2)}, u32[]{:S(2)}) collective-permute-start(f32[128,32]{1,0:T(8,128)S(1)} %bitcast.39), channel_id=1, source_target_pairs={{6,0},{7,1},{4,2},{5,3},{14,8},{15,9},{12,10},{13,11},{22,16},{23,... | collective-permute-start | bytes 49160 | tf_op jit(solution)/shard_map/ppermute | solution.py:73
  156.3 17.9 %collective-permute-start.6 = (f32[128,32]{1,0:T(8,128)S(1)}, f32[128,32]{1,0:T(8,128)S(1)}, u32[]{:S(2)}, u32[]{:S(2)}) collective-permute-start(f32[128,32]{1,0:T(8,128)S(1)} %bitcast.40), channel_id=1, source_target_pairs={{5,0},{6,1},{7,2},{4,3},{13,8},{14,9},{15,10},{12,11},{21,16},{22,... | collective-permute-start | bytes 49160 | tf_op jit(solution)/shard_map/ppermute | solution.py:73
  157.6 18.2 %collective-permute-start.5 = (f32[128,32]{1,0:T(8,128)S(1)}, f32[128,32]{1,0:T(8,128)S(1)}, u32[]{:S(2)}, u32[]{:S(2)}) collective-permute-start(f32[128,32]{1,0:T(8,128)S(1)} %bitcast.41), channel_id=1, source_target_pairs={{4,0},{5,1},{6,2},{7,3},{12,8},{13,9},{14,10},{15,11},{20,16},{21,... | collective-permute-start | bytes 49160 | tf_op jit(solution)/shard_map/ppermute | solution.py:73
  193.9 0.7 collective-permute-start.9
  197.9 9.6 %collective-permute-start.10 = (f32[4,1024]{1,0:T(4,128)S(1)}, f32[4,1024]{1,0:T(4,128)S(1)}, u32[]{:S(2)}, u32[]{:S(2)}) collective-permute-start(f32[4,1024]{1,0:T(4,128)S(1)} %fusion.22), channel_id=1, source_target_pairs={{3,0},{2,1},{11,8},{10,9},{19,16},{18,17},{27,24},{26,25},{35,32},... | collective-permute-start | bytes 49160 | tf_op jit(solution)/shard_map/ppermute | solution.py:59
  210.8 4.5 %collective-permute-start.11 = (f32[4,1024]{1,0:T(4,128)S(1)}, f32[4,1024]{1,0:T(4,128)S(1)}, u32[]{:S(2)}, u32[]{:S(2)}) collective-permute-start(f32[4,1024]{1,0:T(4,128)S(1)} %fusion.4), channel_id=1, source_target_pairs={{3,1},{2,0},{11,9},{10,8},{19,17},{18,16},{27,25},{26,24},{35,33},... | collective-permute-start | bytes 49160 | tf_op jit(solution)/shard_map/ppermute | solution.py:62
  215.3 4.3 %collective-permute-start.12 = (f32[4,1024]{1,0:T(4,128)S(1)}, f32[4,1024]{1,0:T(4,128)S(1)}, u32[]{:S(2)}, u32[]{:S(2)}) collective-permute-start(f32[4,1024]{1,0:T(4,128)S(1)} %select_subtract_fusion), channel_id=1, source_target_pairs={{1,0},{9,8},{17,16},{25,24},{33,32},{41,40},{49,48},{57,56},{65,64... | collective-permute-start | bytes 49160 | tf_op jit(solution)/shard_map/ppermute | solution.py:53
Sparse Core Ops, SparseCore 0:
  20.6 105.4 all-gather.1

commit v2 on v1

v2 whole, which is shorter than its diff:
```python
import jax
import jax.numpy as jnp
from jax import lax
from jax.sharding import PartitionSpec as P


TILE = 128
HALF = 4
DEPTH = 4


def dot(a, b, precision=lax.Precision.HIGHEST):
    return jnp.dot(a, b, precision=precision, preferred_element_type=jnp.float32)


def z_groups(rows):
    return [list(range(y, rows, DEPTH)) for y in range(DEPTH)]


def y_shift(rows, by):
    return [(r // DEPTH * DEPTH + (r + by) % DEPTH, r) for r in range(rows)]


def send_y(array, rows):
    return [array] + [lax.ppermute(array, "row", y_shift(rows, by)) for by in range(1, DEPTH)]


def join_y(parts):
    y = lax.axis_index("row") % DEPTH
    whole = jnp.zeros((DEPTH,) + parts[0].shape, parts[0].dtype)
    for by, part in enumerate(parts):
        whole = lax.dynamic_update_index_in_dim(whole, part, (y + by) % DEPTH, 0)
    return whole


def scatter_z(parts, rows):
    return lax.all_to_all(parts, "row", 0, 0, axis_index_groups=z_groups(rows)).sum(axis=0)


def scatter_rows(partial_sum, rows):
    parts = partial_sum.reshape(rows, -1, partial_sum.shape[1])
    return lax.all_to_all(parts, "row", 0, 0).sum(axis=0)


def on_device(anc_factor, anc_solution, slot_row, tile_count, lower_factor, diag_inverse, rhs):
    column = lax.axis_index("col")
    rows = lax.axis_size("row")
    panels, rows_local, width = lower_factor.shape
    diag = diag_inverse[0]

    scaled = dot(lower_factor.reshape(panels * rows_local, width), diag)
    scaled = scaled.reshape(panels, rows_local, width)
    block = lambda k: lax.dynamic_index_in_dim(scaled, k, 0, keepdims=False)

    own = block(jnp.minimum(column + 1, panels - 1))
    one = block(jnp.where(column < HALF, 2, 7))
    two = block(jnp.where(column < HALF, 3, 6))
    one = lax.ppermute(one, "col", [(5, 7), (4, 3), (0, 6)])
    two = lax.ppermute(two, "col", [(4, 2), (1, 3), (0, 7)])
    upper = jnp.where(column == 2, two, one)
    upper = jnp.where((column >= 4) & (column <= 6), own, upper)
    lower = jnp.where(column == 6, one, two)
    lower = jnp.where(column <= 2, own, lower)

    def near_full(share):
        return lax.all_gather(
            share.reshape(-1, width),
            "row",
            axis=0,
            tiled=True,
            axis_index_groups=z_groups(rows),
        )

    upper = send_y(upper, rows)
    twice = jnp.concatenate([scaled[HALF:], scaled[HALF:-1]], axis=0)
    far = lax.dynamic_slice_in_dim(twice, column % HALF, HALF, 0)
    rest = send_y(jnp.concatenate([lower[None], far], axis=0), rows)
    upper_near = near_full(join_y(upper))

    alive = jnp.arange(slot_row.shape[0]) < tile_count[0] * TILE
    mine = jnp.where(alive[None, :], jnp.take(anc_solution, slot_row, axis=1), 0.0)
    chosen = lax.all_gather(mine, "col", axis=0, tiled=True)
    total = scatter_rows(dot(chosen, anc_factor), rows)
    value = dot(rhs - total, diag)
    value, rest = lax.optimization_barrier((value, rest))
    lower_near = near_full(join_y([lower] + [part[0] for part in rest[1:]]))

    def solve_half(value, low, near):
        a, b, c, d = low, low + 1, low + 2, low + 3
        first, second = (low + 7) % panels, (low + 6) % panels

        def send(array, pairs):
            return lax.ppermute(array, "col", pairs)

        def times(array):
            return dot(array, near, lax.Precision.HIGH)

        got = send(value, [(d, c)]) + send(value, [(d, first)])
        term = times(jnp.where(column == d, value, got))
        value = value - jnp.where(column == c, term, 0.0)
        aside = send(term, [(d, b), (first, a)])
        got = send(value, [(c, b)]) + send(value, [(c, second)])
        term = times(got)
        term, aside = lax.optimization_barrier((term, aside))
        value = value - jnp.where(column == b, term, 0.0) - aside
        aside = send(term, [(second, a)])
        term = times(send(value, [(b, a)]))
        term, aside = lax.optimization_barrier((term, aside))
        return value - term - aside

    value = solve_half(value, HALF, upper_near)
    value, rest = lax.optimization_barrier((value, rest))
    far_full = join_y([far] + [part[1:] for part in rest[1:]]).transpose(1, 0, 2, 3).reshape(-1, width)

    known = []
    for shift in range(HALF):
        pairs = [(HALF + (i + shift) % HALF, i) for i in range(HALF)]
        known.append(lax.ppermute(value, "col", pairs))
    depth = rows // DEPTH
    shares = value.shape[0]
    known = jnp.stack(known).reshape(HALF, shares, depth, -1).transpose(2, 1, 0, 3)
    known = lax.all_to_all(known, "row", 0, 0, axis_index_groups=z_groups(rows))
    term = dot(known.reshape(depth * shares, -1), far_full)
    value = value - scatter_z(term.reshape(depth, shares, width), rows)

    return solve_half(value, 0, lower_near)


def solution(mesh):
    in_specs = (
        P("row", "col"),
        P("col", "row"),
        P("row"),
        P("row"),
        P(None, "row", "col"),
        P("col", None, None),
        P("row", "col"),
    )
    out_specs = P("row", "col")

    return jax.shard_map(
        on_device, mesh=mesh, in_specs=in_specs, out_specs=out_specs, check_vma=False
    )
```

time: 231 us -> 208 us (0.900)
  blocking collectives: 75 us -> 29.7 us
  starting transfers between devices: 18.6 us -> 46.9 us
  waiting for transfers between devices: 78.8 us -> 58.9 us
  local copies, waits for them, and re-layouts: 5.7 us -> 16.2 us
  other arithmetic: 2.02 us -> 6.52 us
  matrix products: 35.7 us -> 32.4 us
    all_to_all x3 -> x1, blocking collectives: 59.8 us -> 10.4 us  [scatter_z(): lax.all_to_all(parts, 'row', 0, 0, axis_index_groups=z_groups(rows))]
    all_gather x1 -> x2, waiting for transfers between devices: 47.5 us -> 0.04 us  [near_full(): lax.all_gather(share.reshape(-1, width), 'row', axis=0, tiled=True, axis_...]
    all_to_all x0 -> x2, waiting for transfers between devices: none -> 20.8 us  [the longest x1 13.8 us: scatter_rows(): return lax.all_to_all(parts, 'row', 0, 0).sum(axis=0)]
    all_to_all x0 -> x2, starting transfers between devices: none -> 14.5 us  [the longest x1 8.77 us: scatter_rows(): return lax.all_to_all(parts, 'row', 0, 0).sum(axis=0)]
    ppermute x13 -> x26, starting transfers between devices: 18.6 us -> 32.4 us  [the longest x14 14.6 us: send(): return lax.ppermute(array, 'col', pairs)]
    dynamic_update_slice x0 -> x9, local copies, waits for them, and re-layouts: none -> 7.95 us  [join_y(): whole = lax.dynamic_update_index_in_dim(whole, part, (y + by) % DEPTH, 0)]
    ppermute x13 -> x26, waiting for transfers between devices: 31.3 us -> 38.1 us  [the longest x6 20.6 us: send_y(): lax.ppermute(array, 'row', y_shift(rows, by))]
    all_gather x1, blocking collectives: 15.3 us -> 19.2 us  [on_device(): chosen = lax.all_gather(mine, 'col', axis=0, tiled=True)]
  transfers between devices with their start and end apart: 14 -> 30, of which waited for: 7 -> 14; matrix products, arithmetic and copies ran while one was open for 6% -> 21% of each run, Pallas kernels for 0% -> 0%
where the time goes in v2:
time: 208 us; the launch traced here: 205 us
  waiting for transfers between devices  58.9 us (28%)
  starting transfers between devices  46.9 us (23%)
  matrix products  32.4 us (16%)
  blocking collectives  29.7 us (14%)
  local copies, waits for them, and re-layouts  16.2 us (8%)
  between operations  14.7 us (7%)
  other arithmetic  6.52 us (3%)
    dot_general x10, matrix products, dot(): jnp.dot(a, b, precision=precision, preferred_element_type=jnp.float32)  32.4 us
    ppermute x6, waiting for transfers between devices, send_y(): lax.ppermute(array, 'row', y_shift(rows, by))  20.6 us
    all_gather x1, blocking collectives, on_device(): chosen = lax.all_gather(mine, 'col', axis=0, tiled=True)  19.2 us
    ppermute x14, starting transfers between devices, send(): return lax.ppermute(array, 'col', pairs)  14.6 us
    all_to_all x1, waiting for transfers between devices, scatter_rows(): return lax.all_to_all(parts, 'row', 0, 0).sum(axis=0)  13.8 us
    ppermute x4, waiting for transfers between devices, on_device(): known.append(lax.ppermute(value, 'col', pairs))  11.1 us
    all_to_all x1, blocking collectives, scatter_z(): lax.all_to_all(parts, 'row', 0, 0, axis_index_groups=z_groups(rows))  10.4 us
    all_to_all x1, starting transfers between devices, scatter_rows(): return lax.all_to_all(parts, 'row', 0, 0).sum(axis=0)  8.77 us
  transfers between devices with their start and end apart: 30, of which 14 were waited for; matrix products, arithmetic and copies ran while one was open for 21% of the time, Pallas kernels for 0%

profile of v2, /device:TPU:1, one launch (start us, length us, event | category | flops | bytes accessed | tf_op | source)
XLA Modules:
  0.0 205.2 jit_solution(4030179027087938778)
XLA Ops:
  6.5 1.2 copy-done
  7.8 5.7 %fusion = f32[256,1024]{1,0:T(8,128)S(1)} fusion(f32[256,1024]{1,0:T(8,128)S(1)} %bitcast.76, f32[1,1024,1024]{2,1,0:T(8,128)} %param.12), kind=kOutput, calls=%fused_computation.1 | convolution fusion | flops 3221225472 | bytes 6291456 | tf_op jit(solution)/shard_map/dot_general | solution.py:13
  13.6 0.7 collective-permute-start
  14.2 4.6 %collective-permute-start.1 = (f32[32,1024]{1,0:T(8,128)S(1)}, f32[32,1024]{1,0:T(8,128)S(1)}, u32[]{:S(2)}, u32[]{:S(2)}) collective-permute-start(f32[32,1024]{1,0:T(8,128)S(1)} %get-tuple-element.43), channel_id=1, source_target_pairs={{4,2},{1,3},{0,7},{12,10},{9,11},{8,15},{20,18},{17,19},{16,23},{2... | collective-permute-start | bytes 393224 | tf_op jit(solution)/shard_map/ppermute | solution.py:59
  18.9 1.9 collective-permute-done.1
  20.8 2.8 %collective-permute-start.7 = (f32[32,1024]{1,0:T(8,128)S(1)}, f32[32,1024]{1,0:T(8,128)S(1)}, u32[]{:S(2)}, u32[]{:S(2)}) collective-permute-start(f32[32,1024]{1,0:T(8,128)S(1)} %get-tuple-element.40), channel_id=1, source_target_pairs={{8,0},{16,8},{24,16},{0,24},{40,32},{48,40},{56,48},{32,56},{72,64... | collective-permute-start | bytes 393224 | tf_op jit(solution)/shard_map/ppermute | solution.py:25
  24.0 0.7 collective-permute-start.9
  24.7 2.3 %collective-permute-done.7 = f32[32,1024]{1,0:T(8,128)S(1)} collective-permute-done((f32[32,1024]{1,0:T(8,128)S(1)}, f32[32,1024]{1,0:T(8,128)S(1)}, u32[]{:S(2)}, u32[]{:S(2)}) %collective-permute-start.7) | collective-permute-done | bytes 131104 | tf_op jit(solution)/shard_map/ppermute | solution.py:25
  27.0 2.1 %collective-permute-done.8 = f32[32,1024]{1,0:T(8,128)S(1)} collective-permute-done((f32[32,1024]{1,0:T(8,128)S(1)}, f32[32,1024]{1,0:T(8,128)S(1)}, u32[]{:S(2)}, u32[]{:S(2)}) %collective-permute-start.8) | collective-permute-done | bytes 131104 | tf_op jit(solution)/shard_map/ppermute | solution.py:25
  29.1 1.3 collective-permute-done.9
  30.4 0.8 copy-done.4
  32.2 2.8 %gather_fusion = f32[1024,16]{1,0:T(8,128)S(1)} fusion(f32[16,1536]{0,1:T(8,128)S(1)} %copy.13, s32[1024]{0:T(1024)S(1)} %fusion.21), kind=kCustom, calls=%fused_computation | custom fusion | bytes 135168 | tf_op jit(solution)/shard_map/jit(_take)/gather | solution.py:81
  35.5 19.2 %all_gather.9 = f32[128,1024]{1,0:T(8,128)S(1)} all-gather(f32[16,1024]{1,0:T(8,128)S(1)} %copy.14), channel_id=1, replica_groups=mesh['row'=32,'col'=8] {'col'}, dimensions={0}, use_global_device_ids=true | all-gather | bytes 589824 | tf_op jit(solution)/shard_map/all_gather | solution.py:82
  54.8 4.6 %fusion.24 = f32[128,1024]{1,0:T(8,128)S(1)} fusion(f32[128,1024]{1,0:T(8,128)S(1)} %all_gather.9, f32[1024,1024]{1,0:T(8,128)} %param.7), kind=kOutput, calls=%fused_computation.54 | convolution fusion | flops 1610612736 | bytes 5242880 | tf_op jit(solution)/shard_map/dot_general | solution.py:13
  59.4 1.0 reshape.44
  60.3 8.8 %all-to-all-start = ((f32[32,4,1024]{2,1,0:T(4,128)}), f32[32,4,1024]{2,1,0:T(4,128)}, u32[]{:S(2)}, u32[]{:S(2)}) async-start(f32[32,4,1024]{2,1,0:T(4,128)} %reshape.44), calls=%async_computation | async-start | bytes 1048576 | tf_op jit(solution)/shard_map/all_to_all | solution.py:42
  69.2 0.8 slice.42
  70.3 1.1 bitcast_dynamic-update-slice_fusion.3
  71.4 0.8 broadcast.16.clone
  72.3 1.7 constant_dynamic-update-slice_fusion
  73.9 0.9 pad_maximum_fusion
  74.8 2.4 %collective-permute-start.2 = (f32[5,32,1024]{2,1,0:T(8,128)}, f32[5,32,1024]{2,1,0:T(8,128)}, u32[]{:S(2)}, u32[]{:S(2)}) collective-permute-start(f32[5,32,1024]{2,1,0:T(8,128)} %pad_maximum_fusion), channel_id=1, source_target_pairs={{8,0},{16,8},{24,16},{0,24},{40,32},{48,40},{56,48},{32,56},{72,64... | collective-permute-start | bytes 1966088 | tf_op jit(solution)/shard_map/ppermute | solution.py:25
  78.4 13.8 %all-to-all-done = f32[32,4,1024]{2,1,0:T(4,128)} async-done(((f32[32,4,1024]{2,1,0:T(4,128)}), f32[32,4,1024]{2,1,0:T(4,128)}, u32[]{:S(2)}, u32[]{:S(2)}) %all-to-all-start) | async-done | bytes 524320 | tf_op jit(solution)/shard_map/all_to_all | solution.py:42
  92.1 1.1 reduce_sum.18
  93.3 4.3 %fusion.2 = f32[4,1024]{1,0:T(4,128)S(1)} fusion(f32[1,1024,1024]{2,1,0:T(8,128)} %param.12, f32[4,1024]{1,0:T(4,128)S(1)} %copy-done.8, f32[4,1024]{1,0:T(4,128)S(1)} %reduce_sum.18), kind=kOutput, calls=%fused_computation.3 | convolution fusion | flops 50335744 | bytes 4243456 | tf_op jit(solution)/shard_map/dot_general | solution.py:13
  98.0 14.5 %collective-permute-done.4 = f32[5,32,1024]{2,1,0:T(8,128)} collective-permute-done((f32[5,32,1024]{2,1,0:T(8,128)}, f32[5,32,1024]{2,1,0:T(8,128)}, u32[]{:S(2)}, u32[]{:S(2)}) %collective-permute-start.4) | collective-permute-done | bytes 655392 | tf_op jit(solution)/shard_map/ppermute | solution.py:25
  112.5 1.6 slice_dynamic-update-slice_fusion.2
  114.1 1.6 slice_dynamic-update-slice_fusion.1
  115.6 1.6 slice_dynamic-update-slice_fusion
  117.2 0.7 collective-permute-start.5
  117.9 0.7 collective-permute-start.6
  118.6 3.3 %select_subtract_fusion.1 = (f32[4,1024]{1,0:T(4,128)S(1)}, f32[4,1024]{1,0:T(4,128)S(1)}) fusion(f32[4,1024]{1,0:T(4,128)S(1)} %fusion.2, pred[]{:T(512)S(6)} %eq.37, f32[1024,1024]{1,0:T(8,128)} %all-gather.3.cloned.1.call-done, f32[4,1024]{1,0:T(4,128)S(1)} %collective-permute-done.5, f32[4,1024]{1,0:T(4,128)S(1)} %collective-permute-done.6, pred[]{:T(512)S(6)} %eq.38), kind=kOutput, calls=%fused_computation.42 | convolution fusion | flops 25182208 | bytes 4276226 | tf_op jit(solution)/shard_map/dot_general | solution.py:13
  122.6 0.7 collective-permute-start.11
  123.3 0.8 collective-permute-start.12
  124.1 3.7 %fusion.13 = f32[4,1024]{1,0:T(4,128)S(1)} fusion(f32[1024,1024]{1,0:T(8,128)} %all-gather.3.cloned.1.call-done, f32[4,1024]{1,0:T(4,128)S(1)} %collective-permute-done.10, f32[4,1024]{1,0:T(4,128)S(1)} %collective-permute-done.11), kind=kOutput, calls=%fused_computation.40 | convolution fusion | flops 25169920 | bytes 4243456 | tf_op jit(solution)/shard_map/dot_general | solution.py:13
  127.8 0.7 collective-permute-start.13
  128.5 0.7 collective-permute-start.14
  129.2 1.4 fusion.25
  130.6 1.3 collective-permute-start.15
  131.9 1.3 collective-permute-start.16
  133.2 1.3 collective-permute-start.17
  134.5 1.3 collective-permute-start.18
  135.8 1.1 bitcast_dynamic-update-slice_fusion.2
  136.9 1.1 bitcast_dynamic-update-slice_fusion.1
  138.0 3.8 %collective-permute-done.15 = f32[4,1024]{1,0:T(4,128)S(1)} collective-permute-done((f32[4,1024]{1,0:T(4,128)S(1)}, f32[4,1024]{1,0:T(4,128)S(1)}, u32[]{:S(2)}, u32[]{:S(2)}) %collective-permute-start.15) | collective-permute-done | bytes 16416 | tf_op jit(solution)/shard_map/ppermute | solution.py:118
  141.8 5.6 %collective-permute-done.16 = f32[4,1024]{1,0:T(4,128)S(1)} collective-permute-done((f32[4,1024]{1,0:T(4,128)S(1)}, f32[4,1024]{1,0:T(4,128)S(1)}, u32[]{:S(2)}, u32[]{:S(2)}) %collective-permute-start.16) | collective-permute-done | bytes 16416 | tf_op jit(solution)/shard_map/ppermute | solution.py:118
  147.4 0.7 collective-permute-done.17
  148.1 0.9 collective-permute-done.18
  149.7 5.8 %all-to-all-start.1 = ((f32[8,4,4,128]{3,1,2,0:T(4,128)}), f32[8,4,4,128]{3,1,2,0:T(4,128)S(1)}, u32[]{:S(2)}, u32[]{:S(2)}) async-start(f32[8,4,4,128]{3,1,2,0:T(4,128)} %maximum_bitcast_fusion), calls=%async_computation.1 | async-start | bytes 131072 | tf_op jit(solution)/shard_map/all_to_all | solution.py:122
  155.5 1.1 bitcast_dynamic-update-slice_fusion
  156.5 7.0 %all-to-all-done.1 = f32[8,4,4,128]{3,1,2,0:T(4,128)S(1)} async-done(((f32[8,4,4,128]{3,1,2,0:T(4,128)}), f32[8,4,4,128]{3,1,2,0:T(4,128)S(1)}, u32[]{:S(2)}, u32[]{:S(2)}) %all-to-all-start.1) | async-done | bytes 65568 | tf_op jit(solution)/shard_map/all_to_all | solution.py:122
  163.5 1.3 fusion.6
  164.9 10.4 %all_to_all.15 = f32[8,4,1024]{2,1,0:T(4,128)S(1)} all-to-all(f32[8,4,1024]{2,1,0:T(4,128)S(1)} %fusion.6), channel_id=1, replica_groups={{0,32,64,96,128,160,192,224},{8,40,72,104,136,168,200,232},{16,48,80,11..., dimensions={0} | all-to-all | bytes 262144 | tf_op jit(solution)/shard_map/all_to_all | solution.py:37
  175.3 0.7 collective-permute-start.19
  176.0 0.7 collective-permute-start.20
  176.7 3.3 %select_subtract_fusion = (f32[4,1024]{1,0:T(4,128)S(1)}, f32[4,1024]{1,0:T(4,128)S(1)}) fusion(f32[4,1024]{1,0:T(4,128)S(1)} %sub.42, pred[]{:T(512)S(6)} %eq.39, f32[1024,1024]{1,0:T(8,128)} %all-gather.5.cloned.1.call-done, f32[4,1024]{1,0:T(4,128)S(1)} %collective-permute-done.19, f32[4,1024]{1,0:T(4,128)S(1)} %collective-permute-done.20, pred[]{:T(512)S(6)} %eq.41), kind=kOutput, calls=%fused_computation.34 | convolution fusion | flops 25182208 | bytes 4276226 | tf_op jit(solution)/shard_map/dot_general | solution.py:13
  180.0 1.3 collective-permute-start.21
  181.3 0.7 collective-permute-start.22
  182.0 1.6 collective-permute-start.23
  183.6 4.3 %collective-permute-done.21 = f32[4,1024]{1,0:T(4,128)S(1)} collective-permute-done((f32[4,1024]{1,0:T(4,128)S(1)}, f32[4,1024]{1,0:T(4,128)S(1)}, u32[]{:S(2)}, u32[]{:S(2)}) %collective-permute-start.21) | collective-permute-done | bytes 16416 | tf_op jit(solution)/shard_map/ppermute | solution.py:93
  187.9 3.3 %fusion.8 = f32[4,1024]{1,0:T(4,128)S(1)} fusion(f32[1024,1024]{1,0:T(8,128)} %all-gather.5.cloned.1.call-done, f32[4,1024]{1,0:T(4,128)S(1)} %collective-permute-done.21, f32[4,1024]{1,0:T(4,128)S(1)} %collective-permute-done.22), kind=kOutput, calls=%fused_computation.32 | convolution fusion | flops 25169920 | bytes 4243456 | tf_op jit(solution)/shard_map/dot_general | solution.py:13
  191.3 4.3 %collective-permute-start.24 = (f32[4,1024]{1,0:T(4,128)S(1)}, f32[4,1024]{1,0:T(4,128)S(1)}, u32[]{:S(2)}, u32[]{:S(2)}) collective-permute-start(f32[4,1024]{1,0:T(4,128)S(1)} %subtract_subtract_fusion.1), channel_id=1, source_target_pairs={{1,0},{9,8},{17,16},{25,24},{33,32},{41,40},{49,48},{57,56},{65,64... | collective-permute-start | bytes 49160 | tf_op jit(solution)/shard_map/ppermute | solution.py:93
  195.6 0.7 collective-permute-start.25
  196.4 1.4 fusion.26
  (65 shorter events, 5.5 us)
Async XLA Ops:
  6.5 1.2 copy-start
  6.5 112.1 %all-gather.3.cloned.1.call-start = ((), (), s32[]{:S(2)}) async-start(), calls=%async_computation.3 | async-start | bytes 4718592 | tf_op jit(solution)/shard_map/all_gather | solution.py:66
  7.8 24.1 %copy-start.7 = (f32[16,1536]{1,0:T(8,128)S(1)}, f32[16,1536]{1,0:T(8,128)}, u32[]{:S(2)}) copy-start(f32[16,1536]{1,0:T(8,128)} %param.8) | copy-start | bytes 294916
  7.8 24.4 %copy-start.9 = (s32[1024]{0:T(1024)S(1)}, s32[1024]{0:T(1024)}, u32[]{:S(2)}) copy-start(s32[1024]{0:T(1024)} %param.9) | copy-start | bytes 12292
  13.5 56.5 %copy-start.3 = (f32[256,1024]{1,0:T(8,128)}, f32[256,1024]{1,0:T(8,128)S(1)}, u32[]{:S(2)}) copy-start(f32[256,1024]{1,0:T(8,128)S(1)} %fusion) | copy-start | bytes 3145732
  13.6 5.3 %collective-permute-start = (f32[32,1024]{1,0:T(8,128)S(1)}, f32[32,1024]{1,0:T(8,128)S(1)}, u32[]{:S(2)}, u32[]{:S(2)}) collective-permute-start(f32[32,1024]{1,0:T(8,128)S(1)} %get-tuple-element.44), channel_id=1, source_target_pairs={{5,7},{4,3},{0,6},{13,15},{12,11},{8,14},{21,23},{20,19},{16,22},{... | collective-permute-start | bytes 393224 | tf_op jit(solution)/shard_map/ppermute | solution.py:58
  14.2 6.5 %collective-permute-start.1 = (f32[32,1024]{1,0:T(8,128)S(1)}, f32[32,1024]{1,0:T(8,128)S(1)}, u32[]{:S(2)}, u32[]{:S(2)}) collective-permute-start(f32[32,1024]{1,0:T(8,128)S(1)} %get-tuple-element.43), channel_id=1, source_target_pairs={{4,2},{1,3},{0,7},{12,10},{9,11},{8,15},{20,18},{17,19},{16,23},{2... | collective-permute-start | bytes 393224 | tf_op jit(solution)/shard_map/ppermute | solution.py:59
  18.9 12.3 %copy-start.5 = (f32[32,1024]{1,0:T(8,128)}, f32[32,1024]{1,0:T(8,128)S(1)}, u32[]{:S(2)}) copy-start(f32[32,1024]{1,0:T(8,128)S(1)} %collective-permute-done) | copy-start | bytes 393220
  20.7 10.5 %copy-start.6 = (f32[32,1024]{1,0:T(8,128)}, f32[32,1024]{1,0:T(8,128)S(1)}, u32[]{:S(2)}) copy-start(f32[32,1024]{1,0:T(8,128)S(1)} %collective-permute-done.1) | copy-start | bytes 393220
  20.8 6.1 %collective-permute-start.7 = (f32[32,1024]{1,0:T(8,128)S(1)}, f32[32,1024]{1,0:T(8,128)S(1)}, u32[]{:S(2)}, u32[]{:S(2)}) collective-permute-start(f32[32,1024]{1,0:T(8,128)S(1)} %get-tuple-element.40), channel_id=1, source_target_pairs={{8,0},{16,8},{24,16},{0,24},{40,32},{48,40},{56,48},{32,56},{72,64... | collective-permute-start | bytes 393224 | tf_op jit(solution)/shard_map/ppermute | solution.py:25
  23.6 5.4 %collective-permute-start.8 = (f32[32,1024]{1,0:T(8,128)S(1)}, f32[32,1024]{1,0:T(8,128)S(1)}, u32[]{:S(2)}, u32[]{:S(2)}) collective-permute-start(f32[32,1024]{1,0:T(8,128)S(1)} %get-tuple-element.40), channel_id=1, source_target_pairs={{16,0},{24,8},{0,16},{8,24},{48,32},{56,40},{32,48},{40,56},{80,64... | collective-permute-start | bytes 393224 | tf_op jit(solution)/shard_map/ppermute | solution.py:25
  24.0 6.4 %collective-permute-start.9 = (f32[32,1024]{1,0:T(8,128)S(1)}, f32[32,1024]{1,0:T(8,128)S(1)}, u32[]{:S(2)}, u32[]{:S(2)}) collective-permute-start(f32[32,1024]{1,0:T(8,128)S(1)} %get-tuple-element.40), channel_id=1, source_target_pairs={{24,0},{0,8},{8,16},{16,24},{56,32},{32,40},{40,48},{48,56},{88,64... | collective-permute-start | bytes 393224 | tf_op jit(solution)/shard_map/ppermute | solution.py:25
  30.4 0.8 copy-start.4
  60.3 31.8 %all-to-all-start = ((f32[32,4,1024]{2,1,0:T(4,128)}), f32[32,4,1024]{2,1,0:T(4,128)}, u32[]{:S(2)}, u32[]{:S(2)}) async-start(f32[32,4,1024]{2,1,0:T(4,128)} %reshape.44), calls=%async_computation | async-start | bytes 1048576 | tf_op jit(solution)/shard_map/all_to_all | solution.py:42
  69.1 107.6 %all-gather.5.cloned.1.call-start = ((), (), s32[]{:S(2)}) async-start(), calls=%async_computation.4 | async-start | bytes 4718592 | tf_op jit(solution)/shard_map/all_gather | solution.py:66
  70.0 23.2 %copy-start.8 = (f32[4,1024]{1,0:T(4,128)S(1)}, f32[4,1024]{1,0:T(4,128)}, u32[]{:S(2)}) copy-start(f32[4,1024]{1,0:T(4,128)} %param.13) | copy-start | bytes 49156
  74.8 22.8 %collective-permute-start.2 = (f32[5,32,1024]{2,1,0:T(8,128)}, f32[5,32,1024]{2,1,0:T(8,128)}, u32[]{:S(2)}, u32[]{:S(2)}) collective-permute-start(f32[5,32,1024]{2,1,0:T(8,128)} %pad_maximum_fusion), channel_id=1, source_target_pairs={{8,0},{16,8},{24,16},{0,24},{40,32},{48,40},{56,48},{32,56},{72,64... | collective-permute-start | bytes 1966088 | tf_op jit(solution)/shard_map/ppermute | solution.py:25
  77.2 20.8 %collective-permute-start.3 = (f32[5,32,1024]{2,1,0:T(8,128)}, f32[5,32,1024]{2,1,0:T(8,128)}, u32[]{:S(2)}, u32[]{:S(2)}) collective-permute-start(f32[5,32,1024]{2,1,0:T(8,128)} %pad_maximum_fusion), channel_id=1, source_target_pairs={{16,0},{24,8},{0,16},{8,24},{48,32},{56,40},{32,48},{40,56},{80,64... | collective-permute-start | bytes 1966088 | tf_op jit(solution)/shard_map/ppermute | solution.py:25
  77.8 34.7 %collective-permute-start.4 = (f32[5,32,1024]{2,1,0:T(8,128)}, f32[5,32,1024]{2,1,0:T(8,128)}, u32[]{:S(2)}, u32[]{:S(2)}) collective-permute-start(f32[5,32,1024]{2,1,0:T(8,128)} %pad_maximum_fusion), channel_id=1, source_target_pairs={{24,0},{0,8},{8,16},{16,24},{56,32},{32,40},{40,48},{48,56},{88,64... | collective-permute-start | bytes 1966088 | tf_op jit(solution)/shard_map/ppermute | solution.py:25
  117.2 1.3 collective-permute-start.5
  117.9 0.7 collective-permute-start.6
  121.9 2.2 %collective-permute-start.10 = (f32[4,1024]{1,0:T(4,128)S(1)}, f32[4,1024]{1,0:T(4,128)S(1)}, u32[]{:S(2)}, u32[]{:S(2)}) collective-permute-start(f32[4,1024]{1,0:T(4,128)S(1)} %get-tuple-element.45), channel_id=1, source_target_pairs={{6,5},{14,13},{22,21},{30,29},{38,37},{46,45},{54,53},{62,61},{70,... | collective-permute-start | bytes 49160 | tf_op jit(solution)/shard_map/ppermute | solution.py:93
  122.6 1.5 collective-permute-start.11
  123.3 5.9 %copy-start.2 = (f32[1024,1024]{1,0:T(8,128)S(1)}, f32[1024,1024]{1,0:T(8,128)}, u32[]{:S(2)}) copy-start(f32[1024,1024]{1,0:T(8,128)} %all-gather.3.cloned.1.call-done) | copy-start | bytes 12582916
  123.3 4.5 %collective-permute-start.12 = (f32[4,1024]{1,0:T(4,128)S(1)}, f32[4,1024]{1,0:T(4,128)S(1)}, u32[]{:S(2)}, u32[]{:S(2)}) collective-permute-start(f32[4,1024]{1,0:T(4,128)S(1)} %get-tuple-element.46), channel_id=1, source_target_pairs={{7,5},{3,4},{15,13},{11,12},{23,21},{19,20},{31,29},{27,28},{39,37... | collective-permute-start | bytes 49160 | tf_op jit(solution)/shard_map/ppermute | solution.py:93
  127.8 1.3 collective-permute-start.13
  128.5 2.0 collective-permute-start.14
  130.6 11.2 %collective-permute-start.15 = (f32[4,1024]{1,0:T(4,128)S(1)}, f32[4,1024]{1,0:T(4,128)S(1)}, u32[]{:S(2)}, u32[]{:S(2)}) collective-permute-start(f32[4,1024]{1,0:T(4,128)S(1)} %subtract_subtract_fusion.2), channel_id=1, source_target_pairs={{4,0},{5,1},{6,2},{7,3},{12,8},{13,9},{14,10},{15,11},{20,16},{21,... | collective-permute-start | bytes 49160 | tf_op jit(solution)/shard_map/ppermute | solution.py:118
  131.9 15.5 %collective-permute-start.16 = (f32[4,1024]{1,0:T(4,128)S(1)}, f32[4,1024]{1,0:T(4,128)S(1)}, u32[]{:S(2)}, u32[]{:S(2)}) collective-permute-start(f32[4,1024]{1,0:T(4,128)S(1)} %subtract_subtract_fusion.2), channel_id=1, source_target_pairs={{5,0},{6,1},{7,2},{4,3},{13,8},{14,9},{15,10},{12,11},{21,16},{22,... | collective-permute-start | bytes 49160 | tf_op jit(solution)/shard_map/ppermute | solution.py:118
  133.2 15.0 %collective-permute-start.17 = (f32[4,1024]{1,0:T(4,128)S(1)}, f32[4,1024]{1,0:T(4,128)S(1)}, u32[]{:S(2)}, u32[]{:S(2)}) collective-permute-start(f32[4,1024]{1,0:T(4,128)S(1)} %subtract_subtract_fusion.2), channel_id=1, source_target_pairs={{6,0},{7,1},{4,2},{5,3},{14,8},{15,9},{12,10},{13,11},{22,16},{23,... | collective-permute-start | bytes 49160 | tf_op jit(solution)/shard_map/ppermute | solution.py:118
  134.5 14.6 %collective-permute-start.18 = (f32[4,1024]{1,0:T(4,128)S(1)}, f32[4,1024]{1,0:T(4,128)S(1)}, u32[]{:S(2)}, u32[]{:S(2)}) collective-permute-start(f32[4,1024]{1,0:T(4,128)S(1)} %subtract_subtract_fusion.2), channel_id=1, source_target_pairs={{7,0},{4,1},{5,2},{6,3},{15,8},{12,9},{13,10},{14,11},{23,16},{20,... | collective-permute-start | bytes 49160 | tf_op jit(solution)/shard_map/ppermute | solution.py:118
  149.7 13.8 %all-to-all-start.1 = ((f32[8,4,4,128]{3,1,2,0:T(4,128)}), f32[8,4,4,128]{3,1,2,0:T(4,128)S(1)}, u32[]{:S(2)}, u32[]{:S(2)}) async-start(f32[8,4,4,128]{3,1,2,0:T(4,128)} %maximum_bitcast_fusion), calls=%async_computation.1 | async-start | bytes 131072 | tf_op jit(solution)/shard_map/all_to_all | solution.py:122
  175.3 1.3 collective-permute-start.19
  176.0 0.7 collective-permute-start.20
  180.0 7.9 %collective-permute-start.21 = (f32[4,1024]{1,0:T(4,128)S(1)}, f32[4,1024]{1,0:T(4,128)S(1)}, u32[]{:S(2)}, u32[]{:S(2)}) collective-permute-start(f32[4,1024]{1,0:T(4,128)S(1)} %get-tuple-element.47), channel_id=1, source_target_pairs={{2,1},{10,9},{18,17},{26,25},{34,33},{42,41},{50,49},{58,57},{66,6... | collective-permute-start | bytes 49160 | tf_op jit(solution)/shard_map/ppermute | solution.py:93
  181.3 6.6 %collective-permute-start.22 = (f32[4,1024]{1,0:T(4,128)S(1)}, f32[4,1024]{1,0:T(4,128)S(1)}, u32[]{:S(2)}, u32[]{:S(2)}) collective-permute-start(f32[4,1024]{1,0:T(4,128)S(1)} %get-tuple-element.47), channel_id=1, source_target_pairs={{2,6},{10,14},{18,22},{26,30},{34,38},{42,46},{50,54},{58,62},{66,... | collective-permute-start | bytes 49160 | tf_op jit(solution)/shard_map/ppermute | solution.py:93
  182.0 14.4 %copy-start.1 = (f32[1024,1024]{1,0:T(8,128)S(1)}, f32[1024,1024]{1,0:T(8,128)}, u32[]{:S(2)}) copy-start(f32[1024,1024]{1,0:T(8,128)} %all-gather.5.cloned.1.call-done) | copy-start | bytes 12582916
  182.0 9.2 %collective-permute-start.23 = (f32[4,1024]{1,0:T(4,128)S(1)}, f32[4,1024]{1,0:T(4,128)S(1)}, u32[]{:S(2)}, u32[]{:S(2)}) collective-permute-start(f32[4,1024]{1,0:T(4,128)S(1)} %get-tuple-element.48), channel_id=1, source_target_pairs={{3,1},{7,0},{11,9},{15,8},{19,17},{23,16},{27,25},{31,24},{35,33},... | collective-permute-start | bytes 49160 | tf_op jit(solution)/shard_map/ppermute | solution.py:93
  191.3 5.2 %collective-permute-start.24 = (f32[4,1024]{1,0:T(4,128)S(1)}, f32[4,1024]{1,0:T(4,128)S(1)}, u32[]{:S(2)}, u32[]{:S(2)}) collective-permute-start(f32[4,1024]{1,0:T(4,128)S(1)} %subtract_subtract_fusion.1), channel_id=1, source_target_pairs={{1,0},{9,8},{17,16},{25,24},{33,32},{41,40},{49,48},{57,56},{65,64... | collective-permute-start | bytes 49160 | tf_op jit(solution)/shard_map/ppermute | solution.py:93
  195.6 2.2 %collective-permute-start.25 = (f32[4,1024]{1,0:T(4,128)S(1)}, f32[4,1024]{1,0:T(4,128)S(1)}, u32[]{:S(2)}, u32[]{:S(2)}) collective-permute-start(f32[4,1024]{1,0:T(4,128)S(1)} %fusion.8), channel_id=1, source_target_pairs={{6,0},{14,8},{22,16},{30,24},{38,32},{46,40},{54,48},{62,56},{70,6... | collective-permute-start | bytes 49160 | tf_op jit(solution)/shard_map/ppermute | solution.py:93
Sparse Core Ops, SparseCore 0:
  31.3 71.8 all-gather.2
  117.3 54.2 all-gather.4

commit v3 on v2

--- a/solution.py
+++ b/solution.py
@@ -83,7 +83,7 @@
     total = scatter_rows(dot(chosen, anc_factor), rows)
     value = dot(rhs - total, diag)
     value, rest = lax.optimization_barrier((value, rest))
-    lower_near = near_full(join_y([lower] + [part[0] for part in rest[1:]]))
+    lower_near = near_full(join_y([part[0] for part in rest]))
 
     def solve_half(value, low, near):
         a, b, c, d = low, low + 1, low + 2, low + 3
@@ -101,16 +101,16 @@
         aside = send(term, [(d, b), (first, a)])
         got = send(value, [(c, b)]) + send(value, [(c, second)])
         term = times(got)
+        last = send(term, [(second, a)])
         term, aside = lax.optimization_barrier((term, aside))
         value = value - jnp.where(column == b, term, 0.0) - aside
-        aside = send(term, [(second, a)])
         term = times(send(value, [(b, a)]))
-        term, aside = lax.optimization_barrier((term, aside))
-        return value - term - aside
+        term, last = lax.optimization_barrier((term, last))
+        return value - term - last
 
     value = solve_half(value, HALF, upper_near)
-    value, rest = lax.optimization_barrier((value, rest))
-    far_full = join_y([far] + [part[1:] for part in rest[1:]]).transpose(1, 0, 2, 3).reshape(-1, width)
+    value, far = lax.optimization_barrier((value, [part[1:] for part in rest]))
+    far_full = join_y(far).transpose(1, 0, 2, 3).reshape(-1, width)
 
     known = []
     for shift in range(HALF):

time: 208 us -> 206 us (level)
  waiting for transfers between devices: 58.9 us -> 63.5 us
  other arithmetic: 6.52 us -> 2.92 us
  local copies, waits for them, and re-layouts: 16.2 us -> 13.6 us
    dynamic_update_slice x9 -> x11, local copies, waits for them, and re-layouts: 7.95 us -> 3.16 us  [join_y(): whole = lax.dynamic_update_index_in_dim(whole, part, (y + by) % DEPTH, 0)]
    all_to_all x1, waiting for transfers between devices: 13.8 us -> 18.1 us  [scatter_rows(): return lax.all_to_all(parts, 'row', 0, 0).sum(axis=0)]
    slice x0 -> x5, local copies, waits for them, and re-layouts: none -> 3.04 us  [on_device(): value, far = lax.optimization_barrier((value, [part[1:] for part in rest]))]
    dynamic_update_slice x3 -> x1, other arithmetic: 2.78 us -> 0.03 us  [join_y(): whole = lax.dynamic_update_index_in_dim(whole, part, (y + by) % DEPTH, 0)]
  transfers between devices with their start and end apart: 30 -> 30, of which waited for: 14 -> 13; matrix products, arithmetic and copies ran while one was open for 21% -> 18% of each run, Pallas kernels for 0% -> 0%
where the time goes in v3:
time: 206 us; the launch traced here: 203 us
  waiting for transfers between devices  63.5 us (31%)
  starting transfers between devices  46.6 us (23%)
  matrix products  32.3 us (16%)
  blocking collectives  29.7 us (14%)
  between operations  14.8 us (7%)
  local copies, waits for them, and re-layouts  13.6 us (7%)
  other arithmetic  2.92 us (1%)
    dot_general x10, matrix products, dot(): jnp.dot(a, b, precision=precision, preferred_element_type=jnp.float32)  32.3 us
    all_gather x1, blocking collectives, on_device(): chosen = lax.all_gather(mine, 'col', axis=0, tiled=True)  19.2 us
    ppermute x6, waiting for transfers between devices, send_y(): lax.ppermute(array, 'row', y_shift(rows, by))  19.1 us
    all_to_all x1, waiting for transfers between devices, scatter_rows(): return lax.all_to_all(parts, 'row', 0, 0).sum(axis=0)  18.1 us
    ppermute x14, starting transfers between devices, send(): return lax.ppermute(array, 'col', pairs)  14.7 us
    ppermute x4, waiting for transfers between devices, on_device(): known.append(lax.ppermute(value, 'col', pairs))  12.8 us
    all_to_all x1, blocking collectives, scatter_z(): lax.all_to_all(parts, 'row', 0, 0, axis_index_groups=z_groups(rows))  10.4 us
    all_to_all x1, starting transfers between devices, scatter_rows(): return lax.all_to_all(parts, 'row', 0, 0).sum(axis=0)  8.64 us
  transfers between devices with their start and end apart: 30, of which 13 were waited for; matrix products, arithmetic and copies ran while one was open for 18% of the time, Pallas kernels for 0%

profile of v3, /device:TPU:1, one launch (start us, length us, event | category | flops | bytes accessed | tf_op | source)
XLA Modules:
  0.0 203.4 jit_solution(303265367008080926)
XLA Ops:
  6.5 1.2 copy-done
  7.8 5.7 %fusion = f32[256,1024]{1,0:T(8,128)S(1)} fusion(f32[256,1024]{1,0:T(8,128)S(1)} %bitcast.76, f32[1,1024,1024]{2,1,0:T(8,128)} %param.12), kind=kOutput, calls=%fused_computation.1 | convolution fusion | flops 3221225472 | bytes 6291456 | tf_op jit(solution)/shard_map/dot_general | solution.py:13
  13.5 0.7 collective-permute-start
  14.2 4.6 %collective-permute-start.1 = (f32[32,1024]{1,0:T(8,128)S(1)}, f32[32,1024]{1,0:T(8,128)S(1)}, u32[]{:S(2)}, u32[]{:S(2)}) collective-permute-start(f32[32,1024]{1,0:T(8,128)S(1)} %get-tuple-element.43), channel_id=1, source_target_pairs={{4,2},{1,3},{0,7},{12,10},{9,11},{8,15},{20,18},{17,19},{16,23},{2... | collective-permute-start | bytes 393224 | tf_op jit(solution)/shard_map/ppermute | solution.py:59
  18.9 1.9 collective-permute-done.1
  20.8 2.8 %collective-permute-start.7 = (f32[32,1024]{1,0:T(8,128)S(1)}, f32[32,1024]{1,0:T(8,128)S(1)}, u32[]{:S(2)}, u32[]{:S(2)}) collective-permute-start(f32[32,1024]{1,0:T(8,128)S(1)} %get-tuple-element.42), channel_id=1, source_target_pairs={{8,0},{16,8},{24,16},{0,24},{40,32},{48,40},{56,48},{32,56},{72,64... | collective-permute-start | bytes 393224 | tf_op jit(solution)/shard_map/ppermute | solution.py:25
  24.0 0.7 collective-permute-start.9
  24.7 2.3 %collective-permute-done.7 = f32[32,1024]{1,0:T(8,128)S(1)} collective-permute-done((f32[32,1024]{1,0:T(8,128)S(1)}, f32[32,1024]{1,0:T(8,128)S(1)}, u32[]{:S(2)}, u32[]{:S(2)}) %collective-permute-start.7) | collective-permute-done | bytes 131104 | tf_op jit(solution)/shard_map/ppermute | solution.py:25
  27.0 2.1 %collective-permute-done.8 = f32[32,1024]{1,0:T(8,128)S(1)} collective-permute-done((f32[32,1024]{1,0:T(8,128)S(1)}, f32[32,1024]{1,0:T(8,128)S(1)}, u32[]{:S(2)}, u32[]{:S(2)}) %collective-permute-start.8) | collective-permute-done | bytes 131104 | tf_op jit(solution)/shard_map/ppermute | solution.py:25
  29.1 1.3 collective-permute-done.9
  30.4 0.8 copy-done.4
  32.2 2.8 %gather_fusion = f32[1024,16]{1,0:T(8,128)S(1)} fusion(f32[16,1536]{0,1:T(8,128)S(1)} %copy.14, s32[1024]{0:T(1024)S(1)} %fusion.21), kind=kCustom, calls=%fused_computation | custom fusion | bytes 135168 | tf_op jit(solution)/shard_map/jit(_take)/gather | solution.py:81
  35.5 19.2 %all_gather.9 = f32[128,1024]{1,0:T(8,128)S(1)} all-gather(f32[16,1024]{1,0:T(8,128)S(1)} %copy.15), channel_id=1, replica_groups=mesh['row'=32,'col'=8] {'col'}, dimensions={0}, use_global_device_ids=true | all-gather | bytes 589824 | tf_op jit(solution)/shard_map/all_gather | solution.py:82
  54.7 4.6 %fusion.22 = f32[128,1024]{1,0:T(8,128)S(1)} fusion(f32[128,1024]{1,0:T(8,128)S(1)} %all_gather.9, f32[1024,1024]{1,0:T(8,128)} %param.7), kind=kOutput, calls=%fused_computation.54 | convolution fusion | flops 1610612736 | bytes 5242880 | tf_op jit(solution)/shard_map/dot_general | solution.py:13
  59.4 0.9 reshape.44
  60.3 8.6 %all-to-all-start = ((f32[32,4,1024]{2,1,0:T(4,128)}), f32[32,4,1024]{2,1,0:T(4,128)S(1)}, u32[]{:S(2)}, u32[]{:S(2)}) async-start(f32[32,4,1024]{2,1,0:T(4,128)} %reshape.44), calls=%async_computation | async-start | bytes 1048576 | tf_op jit(solution)/shard_map/all_to_all | solution.py:42
  69.3 0.9 fusion.5
  70.3 2.5 %collective-permute-start.2 = (f32[5,32,1024]{2,1,0:T(8,128)S(1)}, f32[5,32,1024]{2,1,0:T(8,128)}, u32[]{:S(2)}, u32[]{:S(2)}) collective-permute-start(f32[5,32,1024]{2,1,0:T(8,128)S(1)} %pad_maximum_fusion), channel_id=1, source_target_pairs={{8,0},{16,8},{24,16},{0,24},{40,32},{48,40},{56,48},{32,56},{72,64... | collective-permute-start | bytes 1966088 | tf_op jit(solution)/shard_map/ppermute | solution.py:25
  72.8 0.6 collective-permute-start.3
  73.4 0.6 collective-permute-start.4
  73.9 18.1 %all-to-all-done = f32[32,4,1024]{2,1,0:T(4,128)S(1)} async-done(((f32[32,4,1024]{2,1,0:T(4,128)}), f32[32,4,1024]{2,1,0:T(4,128)S(1)}, u32[]{:S(2)}, u32[]{:S(2)}) %all-to-all-start) | async-done | bytes 524320 | tf_op jit(solution)/shard_map/all_to_all | solution.py:42
  92.1 4.3 %fusion.2 = f32[4,1024]{1,0:T(4,128)S(1)} fusion(f32[1,1024,1024]{2,1,0:T(8,128)} %param.12, f32[4,1024]{1,0:T(4,128)S(1)} %copy-done.9, f32[4,1024]{1,0:T(4,128)S(1)} %reduce_sum.18), kind=kOutput, calls=%fused_computation.3 | convolution fusion | flops 50335744 | bytes 4243456 | tf_op jit(solution)/shard_map/dot_general | solution.py:13
  96.4 13.4 %collective-permute-done.4 = f32[5,32,1024]{2,1,0:T(8,128)} collective-permute-done((f32[5,32,1024]{2,1,0:T(8,128)S(1)}, f32[5,32,1024]{2,1,0:T(8,128)}, u32[]{:S(2)}, u32[]{:S(2)}) %collective-permute-start.4) | collective-permute-done | bytes 655392 | tf_op jit(solution)/shard_map/ppermute | solution.py:25
  109.9 0.9 slice_dynamic-update-slice_fusion.2
  110.9 0.9 slice_dynamic-update-slice_fusion
  111.8 0.8 copy-done.5
  112.6 0.7 collective-permute-start.5
  113.3 0.7 collective-permute-start.6
  114.0 3.3 %select_subtract_fusion.1 = (f32[4,1024]{1,0:T(4,128)S(1)}, f32[4,1024]{1,0:T(4,128)S(1)}) fusion(f32[4,1024]{1,0:T(4,128)S(1)} %fusion.2, pred[]{:T(512)S(6)} %eq.37, f32[1024,1024]{1,0:T(8,128)} %all-gather.3.cloned.1.call-done, f32[4,1024]{1,0:T(4,128)S(1)} %collective-permute-done.5, f32[4,1024]{1,0:T(4,128)S(1)} %collective-permute-done.6, pred[]{:T(512)S(6)} %eq.38), kind=kOutput, calls=%fused_computation.43 | convolution fusion | flops 25182208 | bytes 4276226 | tf_op jit(solution)/shard_map/dot_general | solution.py:13
  117.3 0.7 collective-permute-start.10
  118.0 0.7 collective-permute-start.11
  118.7 0.8 collective-permute-start.12
  119.5 3.7 %fusion.13 = f32[4,1024]{1,0:T(4,128)S(1)} fusion(f32[1024,1024]{1,0:T(8,128)} %all-gather.3.cloned.1.call-done, f32[4,1024]{1,0:T(4,128)S(1)} %collective-permute-done.10, f32[4,1024]{1,0:T(4,128)S(1)} %collective-permute-done.11), kind=kOutput, calls=%fused_computation.41 | convolution fusion | flops 25169920 | bytes 4243456 | tf_op jit(solution)/shard_map/dot_general | solution.py:13
  123.2 0.7 collective-permute-start.13
  123.9 1.1 slice.41
  125.0 1.9 slice.43
  127.0 0.8 collective-permute-start.14
  127.8 1.4 fusion.23
  129.2 1.3 collective-permute-start.15
  130.4 1.3 collective-permute-start.16
  131.8 1.3 collective-permute-start.17
  133.1 1.3 collective-permute-start.18
  134.8 5.5 %collective-permute-done.15 = f32[4,1024]{1,0:T(4,128)S(1)} collective-permute-done((f32[4,1024]{1,0:T(4,128)S(1)}, f32[4,1024]{1,0:T(4,128)S(1)}, u32[]{:S(2)}, u32[]{:S(2)}) %collective-permute-start.15) | collective-permute-done | bytes 16416 | tf_op jit(solution)/shard_map/ppermute | solution.py:118
  140.3 5.7 %collective-permute-done.16 = f32[4,1024]{1,0:T(4,128)S(1)} collective-permute-done((f32[4,1024]{1,0:T(4,128)S(1)}, f32[4,1024]{1,0:T(4,128)S(1)}, u32[]{:S(2)}, u32[]{:S(2)}) %collective-permute-start.16) | collective-permute-done | bytes 16416 | tf_op jit(solution)/shard_map/ppermute | solution.py:118
  146.0 0.7 collective-permute-done.17
  146.7 0.9 collective-permute-done.18
  147.7 0.6 maximum_bitcast_fusion
  148.3 5.3 %all-to-all-start.1 = ((f32[8,4,4,128]{3,1,2,0:T(4,128)}), f32[8,4,4,128]{3,1,2,0:T(4,128)S(1)}, u32[]{:S(2)}, u32[]{:S(2)}) async-start(f32[8,4,4,128]{3,1,2,0:T(4,128)} %maximum_bitcast_fusion), calls=%async_computation.1 | async-start | bytes 131072 | tf_op jit(solution)/shard_map/all_to_all | solution.py:122
  153.6 1.1 bitcast_dynamic-update-slice_fusion
  154.7 7.0 %all-to-all-done.1 = f32[8,4,4,128]{3,1,2,0:T(4,128)S(1)} async-done(((f32[8,4,4,128]{3,1,2,0:T(4,128)}), f32[8,4,4,128]{3,1,2,0:T(4,128)S(1)}, u32[]{:S(2)}, u32[]{:S(2)}) %all-to-all-start.1) | async-done | bytes 65568 | tf_op jit(solution)/shard_map/all_to_all | solution.py:122
  161.7 1.3 fusion.6
  163.0 10.4 %all_to_all.15 = f32[8,4,1024]{2,1,0:T(4,128)S(1)} all-to-all(f32[8,4,1024]{2,1,0:T(4,128)S(1)} %fusion.6), channel_id=1, replica_groups={{0,32,64,96,128,160,192,224},{8,40,72,104,136,168,200,232},{16,48,80,11..., dimensions={0} | all-to-all | bytes 262144 | tf_op jit(solution)/shard_map/all_to_all | solution.py:37
  173.4 0.7 collective-permute-start.19
  174.1 0.7 collective-permute-start.20
  174.8 3.3 %select_subtract_fusion = (f32[4,1024]{1,0:T(4,128)S(1)}, f32[4,1024]{1,0:T(4,128)S(1)}) fusion(f32[4,1024]{1,0:T(4,128)S(1)} %sub.42, pred[]{:T(512)S(6)} %eq.39, f32[1024,1024]{1,0:T(8,128)} %all-gather.5.cloned.1.call-done, f32[4,1024]{1,0:T(4,128)S(1)} %collective-permute-done.19, f32[4,1024]{1,0:T(4,128)S(1)} %collective-permute-done.20, pred[]{:T(512)S(6)} %eq.41), kind=kOutput, calls=%fused_computation.35 | convolution fusion | flops 25182208 | bytes 4276226 | tf_op jit(solution)/shard_map/dot_general | solution.py:13
  178.1 1.3 collective-permute-start.21
  179.4 0.7 collective-permute-start.22
  180.1 1.6 collective-permute-start.23
  181.7 4.4 %collective-permute-done.21 = f32[4,1024]{1,0:T(4,128)S(1)} collective-permute-done((f32[4,1024]{1,0:T(4,128)S(1)}, f32[4,1024]{1,0:T(4,128)S(1)}, u32[]{:S(2)}, u32[]{:S(2)}) %collective-permute-start.21) | collective-permute-done | bytes 16416 | tf_op jit(solution)/shard_map/ppermute | solution.py:93
  186.0 3.3 %fusion.8 = f32[4,1024]{1,0:T(4,128)S(1)} fusion(f32[1024,1024]{1,0:T(8,128)} %all-gather.5.cloned.1.call-done, f32[4,1024]{1,0:T(4,128)S(1)} %collective-permute-done.21, f32[4,1024]{1,0:T(4,128)S(1)} %collective-permute-done.22), kind=kOutput, calls=%fused_computation.33 | convolution fusion | flops 25169920 | bytes 4243456 | tf_op jit(solution)/shard_map/dot_general | solution.py:13
  189.4 4.3 %collective-permute-start.24 = (f32[4,1024]{1,0:T(4,128)S(1)}, f32[4,1024]{1,0:T(4,128)S(1)}, u32[]{:S(2)}, u32[]{:S(2)}) collective-permute-start(f32[4,1024]{1,0:T(4,128)S(1)} %subtract_subtract_fusion.1), channel_id=1, source_target_pairs={{1,0},{9,8},{17,16},{25,24},{33,32},{41,40},{49,48},{57,56},{65,64... | collective-permute-start | bytes 49160 | tf_op jit(solution)/shard_map/ppermute | solution.py:93
  193.7 0.7 collective-permute-start.25
  194.5 1.4 fusion.24
  195.9 0.6 subtract_subtract_fusion
  (74 shorter events, 2.6 us)
Async XLA Ops:
  6.5 1.2 copy-start
  6.5 107.4 %all-gather.3.cloned.1.call-start = ((), (), s32[]{:S(2)}) async-start(), calls=%async_computation.3 | async-start | bytes 4718592 | tf_op jit(solution)/shard_map/all_gather | solution.py:66
  7.8 24.1 %copy-start.8 = (f32[16,1536]{1,0:T(8,128)S(1)}, f32[16,1536]{1,0:T(8,128)}, u32[]{:S(2)}) copy-start(f32[16,1536]{1,0:T(8,128)} %param.8) | copy-start | bytes 294916
  7.8 24.4 %copy-start.10 = (s32[1024]{0:T(1024)S(1)}, s32[1024]{0:T(1024)}, u32[]{:S(2)}) copy-start(s32[1024]{0:T(1024)} %param.9) | copy-start | bytes 12292
  13.5 5.3 %collective-permute-start = (f32[32,1024]{1,0:T(8,128)S(1)}, f32[32,1024]{1,0:T(8,128)S(1)}, u32[]{:S(2)}, u32[]{:S(2)}) collective-permute-start(f32[32,1024]{1,0:T(8,128)S(1)} %get-tuple-element.44), channel_id=1, source_target_pairs={{5,7},{4,3},{0,6},{13,15},{12,11},{8,14},{21,23},{20,19},{16,22},{... | collective-permute-start | bytes 393224 | tf_op jit(solution)/shard_map/ppermute | solution.py:58
  14.2 6.5 %collective-permute-start.1 = (f32[32,1024]{1,0:T(8,128)S(1)}, f32[32,1024]{1,0:T(8,128)S(1)}, u32[]{:S(2)}, u32[]{:S(2)}) collective-permute-start(f32[32,1024]{1,0:T(8,128)S(1)} %get-tuple-element.43), channel_id=1, source_target_pairs={{4,2},{1,3},{0,7},{12,10},{9,11},{8,15},{20,18},{17,19},{16,23},{2... | collective-permute-start | bytes 393224 | tf_op jit(solution)/shard_map/ppermute | solution.py:59
  18.9 12.3 %copy-start.6 = (f32[32,1024]{1,0:T(8,128)}, f32[32,1024]{1,0:T(8,128)S(1)}, u32[]{:S(2)}) copy-start(f32[32,1024]{1,0:T(8,128)S(1)} %collective-permute-done) | copy-start | bytes 393220
  20.7 10.5 %copy-start.7 = (f32[32,1024]{1,0:T(8,128)}, f32[32,1024]{1,0:T(8,128)S(1)}, u32[]{:S(2)}) copy-start(f32[32,1024]{1,0:T(8,128)S(1)} %collective-permute-done.1) | copy-start | bytes 393220
  20.8 6.1 %collective-permute-start.7 = (f32[32,1024]{1,0:T(8,128)S(1)}, f32[32,1024]{1,0:T(8,128)S(1)}, u32[]{:S(2)}, u32[]{:S(2)}) collective-permute-start(f32[32,1024]{1,0:T(8,128)S(1)} %get-tuple-element.42), channel_id=1, source_target_pairs={{8,0},{16,8},{24,16},{0,24},{40,32},{48,40},{56,48},{32,56},{72,64... | collective-permute-start | bytes 393224 | tf_op jit(solution)/shard_map/ppermute | solution.py:25
  23.6 5.4 %collective-permute-start.8 = (f32[32,1024]{1,0:T(8,128)S(1)}, f32[32,1024]{1,0:T(8,128)S(1)}, u32[]{:S(2)}, u32[]{:S(2)}) collective-permute-start(f32[32,1024]{1,0:T(8,128)S(1)} %get-tuple-element.42), channel_id=1, source_target_pairs={{16,0},{24,8},{0,16},{8,24},{48,32},{56,40},{32,48},{40,56},{80,64... | collective-permute-start | bytes 393224 | tf_op jit(solution)/shard_map/ppermute | solution.py:25
  24.0 6.4 %collective-permute-start.9 = (f32[32,1024]{1,0:T(8,128)S(1)}, f32[32,1024]{1,0:T(8,128)S(1)}, u32[]{:S(2)}, u32[]{:S(2)}) collective-permute-start(f32[32,1024]{1,0:T(8,128)S(1)} %get-tuple-element.42), channel_id=1, source_target_pairs={{24,0},{0,8},{8,16},{16,24},{56,32},{32,40},{40,48},{48,56},{88,64... | collective-permute-start | bytes 393224 | tf_op jit(solution)/shard_map/ppermute | solution.py:25
  30.4 0.8 copy-start.4
  59.4 32.7 %copy-start.9 = (f32[4,1024]{1,0:T(4,128)S(1)}, f32[4,1024]{1,0:T(4,128)}, u32[]{:S(2)}) copy-start(f32[4,1024]{1,0:T(4,128)} %param.13) | copy-start | bytes 49156
  60.3 31.7 %all-to-all-start = ((f32[32,4,1024]{2,1,0:T(4,128)}), f32[32,4,1024]{2,1,0:T(4,128)S(1)}, u32[]{:S(2)}, u32[]{:S(2)}) async-start(f32[32,4,1024]{2,1,0:T(4,128)} %reshape.44), calls=%async_computation | async-start | bytes 1048576 | tf_op jit(solution)/shard_map/all_to_all | solution.py:42
  69.0 105.8 %all-gather.5.cloned.1.call-start = ((), (), s32[]{:S(2)}) async-start(), calls=%async_computation.4 | async-start | bytes 4718592 | tf_op jit(solution)/shard_map/all_gather | solution.py:66
  70.3 26.1 %collective-permute-start.2 = (f32[5,32,1024]{2,1,0:T(8,128)S(1)}, f32[5,32,1024]{2,1,0:T(8,128)}, u32[]{:S(2)}, u32[]{:S(2)}) collective-permute-start(f32[5,32,1024]{2,1,0:T(8,128)S(1)} %pad_maximum_fusion), channel_id=1, source_target_pairs={{8,0},{16,8},{24,16},{0,24},{40,32},{48,40},{56,48},{32,56},{72,64... | collective-permute-start | bytes 1966088 | tf_op jit(solution)/shard_map/ppermute | solution.py:25
  72.8 23.6 %collective-permute-start.3 = (f32[5,32,1024]{2,1,0:T(8,128)S(1)}, f32[5,32,1024]{2,1,0:T(8,128)S(1)}, u32[]{:S(2)}, u32[]{:S(2)}) collective-permute-start(f32[5,32,1024]{2,1,0:T(8,128)S(1)} %pad_maximum_fusion), channel_id=1, source_target_pairs={{16,0},{24,8},{0,16},{8,24},{48,32},{56,40},{32,48},{40,56},{80,64... | collective-permute-start | bytes 1966088 | tf_op jit(solution)/shard_map/ppermute | solution.py:25
  73.4 36.5 %collective-permute-start.4 = (f32[5,32,1024]{2,1,0:T(8,128)S(1)}, f32[5,32,1024]{2,1,0:T(8,128)}, u32[]{:S(2)}, u32[]{:S(2)}) collective-permute-start(f32[5,32,1024]{2,1,0:T(8,128)S(1)} %pad_maximum_fusion), channel_id=1, source_target_pairs={{24,0},{0,8},{8,16},{16,24},{56,32},{32,40},{40,48},{48,56},{88,64... | collective-permute-start | bytes 1966088 | tf_op jit(solution)/shard_map/ppermute | solution.py:25
  96.4 28.6 %copy-start.3 = (f32[5,32,1024]{2,1,0:T(8,128)}, f32[5,32,1024]{2,1,0:T(8,128)S(1)}, u32[]{:S(2)}) copy-start(f32[5,32,1024]{2,1,0:T(8,128)S(1)} %collective-permute-done.3) | copy-start | bytes 1966084
  111.8 0.8 copy-start.5
  112.6 1.3 collective-permute-start.5
  113.3 0.7 collective-permute-start.6
  117.3 2.2 %collective-permute-start.10 = (f32[4,1024]{1,0:T(4,128)S(1)}, f32[4,1024]{1,0:T(4,128)S(1)}, u32[]{:S(2)}, u32[]{:S(2)}) collective-permute-start(f32[4,1024]{1,0:T(4,128)S(1)} %get-tuple-element.45), channel_id=1, source_target_pairs={{6,5},{14,13},{22,21},{30,29},{38,37},{46,45},{54,53},{62,61},{70,... | collective-permute-start | bytes 49160 | tf_op jit(solution)/shard_map/ppermute | solution.py:93
  118.0 1.5 collective-permute-start.11
  118.7 9.1 %copy-start.2 = (f32[1024,1024]{1,0:T(8,128)S(1)}, f32[1024,1024]{1,0:T(8,128)}, u32[]{:S(2)}) copy-start(f32[1024,1024]{1,0:T(8,128)} %all-gather.3.cloned.1.call-done) | copy-start | bytes 12582916
  118.7 4.5 %collective-permute-start.12 = (f32[4,1024]{1,0:T(4,128)S(1)}, f32[4,1024]{1,0:T(4,128)S(1)}, u32[]{:S(2)}, u32[]{:S(2)}) collective-permute-start(f32[4,1024]{1,0:T(4,128)S(1)} %get-tuple-element.46), channel_id=1, source_target_pairs={{7,5},{3,4},{15,13},{11,12},{23,21},{19,20},{31,29},{27,28},{39,37... | collective-permute-start | bytes 49160 | tf_op jit(solution)/shard_map/ppermute | solution.py:93
  123.2 4.5 %collective-permute-start.13 = (f32[4,1024]{1,0:T(4,128)S(1)}, f32[4,1024]{1,0:T(4,128)S(1)}, u32[]{:S(2)}, u32[]{:S(2)}) collective-permute-start(f32[4,1024]{1,0:T(4,128)S(1)} %subtract_subtract_fusion.3), channel_id=1, source_target_pairs={{5,4},{13,12},{21,20},{29,28},{37,36},{45,44},{53,52},{61,60},{69,... | collective-permute-start | bytes 49160 | tf_op jit(solution)/shard_map/ppermute | solution.py:93
  127.0 7.8 %slice-start = ((f32[5,32,1024]{2,1,0:T(8,128)}), f32[4,32,1024]{2,1,0:T(8,128)S(1)}, s32[]{:S(2)}) async-start(f32[5,32,1024]{2,1,0:T(8,128)} %copy-done.3), calls=%async_computation.5 | async-start | bytes 1048576 | tf_op jit(solution)/shard_map/slice | solution.py:112
  127.0 2.2 %collective-permute-start.14 = (f32[4,1024]{1,0:T(4,128)S(1)}, f32[4,1024]{1,0:T(4,128)S(1)}, u32[]{:S(2)}, u32[]{:S(2)}) collective-permute-start(f32[4,1024]{1,0:T(4,128)S(1)} %fusion.13), channel_id=1, source_target_pairs={{2,4},{10,12},{18,20},{26,28},{34,36},{42,44},{50,52},{58,60},{66,... | collective-permute-start | bytes 49160 | tf_op jit(solution)/shard_map/ppermute | solution.py:93
  129.2 11.1 %collective-permute-start.15 = (f32[4,1024]{1,0:T(4,128)S(1)}, f32[4,1024]{1,0:T(4,128)S(1)}, u32[]{:S(2)}, u32[]{:S(2)}) collective-permute-start(f32[4,1024]{1,0:T(4,128)S(1)} %subtract_subtract_fusion.2), channel_id=1, source_target_pairs={{4,0},{5,1},{6,2},{7,3},{12,8},{13,9},{14,10},{15,11},{20,16},{21,... | collective-permute-start | bytes 49160 | tf_op jit(solution)/shard_map/ppermute | solution.py:118
  130.4 15.6 %collective-permute-start.16 = (f32[4,1024]{1,0:T(4,128)S(1)}, f32[4,1024]{1,0:T(4,128)S(1)}, u32[]{:S(2)}, u32[]{:S(2)}) collective-permute-start(f32[4,1024]{1,0:T(4,128)S(1)} %subtract_subtract_fusion.2), channel_id=1, source_target_pairs={{5,0},{6,1},{7,2},{4,3},{13,8},{14,9},{15,10},{12,11},{21,16},{22,... | collective-permute-start | bytes 49160 | tf_op jit(solution)/shard_map/ppermute | solution.py:118
  131.8 15.0 %collective-permute-start.17 = (f32[4,1024]{1,0:T(4,128)S(1)}, f32[4,1024]{1,0:T(4,128)S(1)}, u32[]{:S(2)}, u32[]{:S(2)}) collective-permute-start(f32[4,1024]{1,0:T(4,128)S(1)} %subtract_subtract_fusion.2), channel_id=1, source_target_pairs={{6,0},{7,1},{4,2},{5,3},{14,8},{15,9},{12,10},{13,11},{22,16},{23,... | collective-permute-start | bytes 49160 | tf_op jit(solution)/shard_map/ppermute | solution.py:118
  133.1 14.6 %collective-permute-start.18 = (f32[4,1024]{1,0:T(4,128)S(1)}, f32[4,1024]{1,0:T(4,128)S(1)}, u32[]{:S(2)}, u32[]{:S(2)}) collective-permute-start(f32[4,1024]{1,0:T(4,128)S(1)} %subtract_subtract_fusion.2), channel_id=1, source_target_pairs={{7,0},{4,1},{5,2},{6,3},{15,8},{12,9},{13,10},{14,11},{23,16},{20,... | collective-permute-start | bytes 49160 | tf_op jit(solution)/shard_map/ppermute | solution.py:118
  148.3 13.3 %all-to-all-start.1 = ((f32[8,4,4,128]{3,1,2,0:T(4,128)}), f32[8,4,4,128]{3,1,2,0:T(4,128)S(1)}, u32[]{:S(2)}, u32[]{:S(2)}) async-start(f32[8,4,4,128]{3,1,2,0:T(4,128)} %maximum_bitcast_fusion), calls=%async_computation.1 | async-start | bytes 131072 | tf_op jit(solution)/shard_map/all_to_all | solution.py:122
  173.4 1.3 collective-permute-start.19
  174.1 0.7 collective-permute-start.20
  178.1 7.9 %collective-permute-start.21 = (f32[4,1024]{1,0:T(4,128)S(1)}, f32[4,1024]{1,0:T(4,128)S(1)}, u32[]{:S(2)}, u32[]{:S(2)}) collective-permute-start(f32[4,1024]{1,0:T(4,128)S(1)} %get-tuple-element.47), channel_id=1, source_target_pairs={{2,1},{10,9},{18,17},{26,25},{34,33},{42,41},{50,49},{58,57},{66,6... | collective-permute-start | bytes 49160 | tf_op jit(solution)/shard_map/ppermute | solution.py:93
  179.4 6.6 %collective-permute-start.22 = (f32[4,1024]{1,0:T(4,128)S(1)}, f32[4,1024]{1,0:T(4,128)S(1)}, u32[]{:S(2)}, u32[]{:S(2)}) collective-permute-start(f32[4,1024]{1,0:T(4,128)S(1)} %get-tuple-element.47), channel_id=1, source_target_pairs={{2,6},{10,14},{18,22},{26,30},{34,38},{42,46},{50,54},{58,62},{66,... | collective-permute-start | bytes 49160 | tf_op jit(solution)/shard_map/ppermute | solution.py:93
  180.1 14.4 %copy-start.1 = (f32[1024,1024]{1,0:T(8,128)S(1)}, f32[1024,1024]{1,0:T(8,128)}, u32[]{:S(2)}) copy-start(f32[1024,1024]{1,0:T(8,128)} %all-gather.5.cloned.1.call-done) | copy-start | bytes 12582916
  180.1 9.2 %collective-permute-start.23 = (f32[4,1024]{1,0:T(4,128)S(1)}, f32[4,1024]{1,0:T(4,128)S(1)}, u32[]{:S(2)}, u32[]{:S(2)}) collective-permute-start(f32[4,1024]{1,0:T(4,128)S(1)} %get-tuple-element.48), channel_id=1, source_target_pairs={{3,1},{7,0},{11,9},{15,8},{19,17},{23,16},{27,25},{31,24},{35,33},... | collective-permute-start | bytes 49160 | tf_op jit(solution)/shard_map/ppermute | solution.py:93
  189.4 5.2 %collective-permute-start.24 = (f32[4,1024]{1,0:T(4,128)S(1)}, f32[4,1024]{1,0:T(4,128)S(1)}, u32[]{:S(2)}, u32[]{:S(2)}) collective-permute-start(f32[4,1024]{1,0:T(4,128)S(1)} %subtract_subtract_fusion.1), channel_id=1, source_target_pairs={{1,0},{9,8},{17,16},{25,24},{33,32},{41,40},{49,48},{57,56},{65,64... | collective-permute-start | bytes 49160 | tf_op jit(solution)/shard_map/ppermute | solution.py:93
  193.7 2.2 %collective-permute-start.25 = (f32[4,1024]{1,0:T(4,128)S(1)}, f32[4,1024]{1,0:T(4,128)S(1)}, u32[]{:S(2)}, u32[]{:S(2)}) collective-permute-start(f32[4,1024]{1,0:T(4,128)S(1)} %fusion.8), channel_id=1, source_target_pairs={{6,0},{14,8},{22,16},{30,24},{38,32},{46,40},{54,48},{62,56},{70,6... | collective-permute-start | bytes 49160 | tf_op jit(solution)/shard_map/ppermute | solution.py:93
Sparse Core Ops, SparseCore 0:
  31.3 71.8 all-gather.2
  112.7 54.0 all-gather.4

commit v4 on v3

--- a/solution.py
+++ b/solution.py
@@ -25,6 +25,17 @@
     return [array] + [lax.ppermute(array, "row", y_shift(rows, by)) for by in range(1, DEPTH)]
 
 
+def order_y(parts):
+    y = lax.axis_index("row") % DEPTH
+    rows = []
+    for place in range(DEPTH):
+        row = parts[place]
+        for at in range(1, DEPTH):
+            row = jnp.where(y == at, parts[(place - at) % DEPTH], row)
+        rows.append(row)
+    return jnp.stack(rows)
+
+
 def join_y(parts):
     y = lax.axis_index("row") % DEPTH
     whole = jnp.zeros((DEPTH,) + parts[0].shape, parts[0].dtype)
@@ -37,9 +48,14 @@
     return lax.all_to_all(parts, "row", 0, 0, axis_index_groups=z_groups(rows)).sum(axis=0)
 
 
-def scatter_rows(partial_sum, rows):
-    parts = partial_sum.reshape(rows, -1, partial_sum.shape[1])
-    return lax.all_to_all(parts, "row", 0, 0).sum(axis=0)
+def scatter_y(partial_sum, rows):
+    y = lax.axis_index("row") % DEPTH
+    parts = partial_sum.reshape(rows // DEPTH, DEPTH, -1, partial_sum.shape[1])
+    total = lax.dynamic_index_in_dim(parts, y, 1, keepdims=False)
+    for by in range(1, DEPTH):
+        give = lax.dynamic_index_in_dim(parts, (y + DEPTH - by) % DEPTH, 1, keepdims=False)
+        total = total + lax.ppermute(give, "row", y_shift(rows, by))
+    return total
 
 
 def on_device(anc_factor, anc_solution, slot_row, tile_count, lower_factor, diag_inverse, rhs):
@@ -72,18 +88,25 @@
         )
 
     upper = send_y(upper, rows)
+    lower = send_y(lower, rows)
+    upper_near = near_full(order_y(upper))
+
+    alive = jnp.arange(slot_row.shape[0]) < tile_count[0] * TILE
+    slot = jnp.where(alive, slot_row, -1)
+    chooser = jnp.arange(anc_solution.shape[1])[:, None] == slot[None, :]
+    mine = dot(anc_solution, chooser.astype(jnp.float32))
+    chosen = lax.all_gather(mine, "col", axis=0, tiled=True)
+    term = dot(chosen, anc_factor)
+    term, lower = lax.optimization_barrier((term, lower))
+    lower = order_y(lower)
+    lower_near = near_full(lower)
+    total = scatter_y(term, rows)
     twice = jnp.concatenate([scaled[HALF:], scaled[HALF:-1]], axis=0)
     far = lax.dynamic_slice_in_dim(twice, column % HALF, HALF, 0)
-    rest = send_y(jnp.concatenate([lower[None], far], axis=0), rows)
-    upper_near = near_full(join_y(upper))
-
-    alive = jnp.arange(slot_row.shape[0]) < tile_count[0] * TILE
-    mine = jnp.where(alive[None, :], jnp.take(anc_solution, slot_row, axis=1), 0.0)
-    chosen = lax.all_gather(mine, "col", axis=0, tiled=True)
-    total = scatter_rows(dot(chosen, anc_factor), rows)
+    total, far = lax.optimization_barrier((total, far))
+    far = send_y(far, rows)
+    total = scatter_z(total, rows)
     value = dot(rhs - total, diag)
-    value, rest = lax.optimization_barrier((value, rest))
-    lower_near = near_full(join_y([part[0] for part in rest]))
 
     def solve_half(value, low, near):
         a, b, c, d = low, low + 1, low + 2, low + 3
@@ -109,7 +132,7 @@
         return value - term - last
 
     value = solve_half(value, HALF, upper_near)
-    value, far = lax.optimization_barrier((value, [part[1:] for part in rest]))
+    value, far = lax.optimization_barrier((value, far))
     far_full = join_y(far).transpose(1, 0, 2, 3).reshape(-1, width)
 
     known = []
@@ -120,7 +143,7 @@
     shares = value.shape[0]
     known = jnp.stack(known).reshape(HALF, shares, depth, -1).transpose(2, 1, 0, 3)
     known = lax.all_to_all(known, "row", 0, 0, axis_index_groups=z_groups(rows))
-    term = dot(known.reshape(depth * shares, -1), far_full)
+    term = dot(known.reshape(depth * shares, -1), far_full, lax.Precision.HIGH)
     value = value - scatter_z(term.reshape(depth, shares, width), rows)
 
     return solve_half(value, 0, lower_near)

time: 206 us -> 209 us (1.015)
  blocking collectives: 29.7 us -> 48 us
  local copies, waits for them, and re-layouts: 13.6 us -> 3.81 us
  starting transfers between devices: 46.6 us -> 36.9 us
  matrix products: 32.3 us -> 35.5 us
    all_to_all x1 -> x2, blocking collectives: 10.4 us -> 28.7 us  [scatter_z(): lax.all_to_all(parts, 'row', 0, 0, axis_index_groups=z_groups(rows))]
    all_to_all x1 -> x0, waiting for transfers between devices: 18.1 us -> none  [scatter_rows(): return lax.all_to_all(parts, 'row', 0, 0).sum(axis=0)]
    ppermute x6 -> x9, waiting for transfers between devices: 19.1 us -> 30.9 us  [send_y(): lax.ppermute(array, 'row', y_shift(rows, by))]
    all_to_all x1 -> x0, starting transfers between devices: 8.64 us -> none  [scatter_rows(): return lax.all_to_all(parts, 'row', 0, 0).sum(axis=0)]
    ppermute x0 -> x3, waiting for transfers between devices: none -> 8.19 us  [scatter_y(): total = total + lax.ppermute(give, 'row', y_shift(rows, by))]
    dot_general x10 -> x11, matrix products: 32.3 us -> 35.5 us  [dot(): jnp.dot(a, b, precision=precision, preferred_element_type=jnp.float32)]
    slice x5 -> x0, local copies, waits for them, and re-layouts: 3.04 us -> none  [on_device(): value, far = lax.optimization_barrier((value, [part[1:] for part in rest]))]
    gather x1 -> x0, local copies, waits for them, and re-layouts: 2.81 us -> none  [on_device(): jnp.take(anc_solution, slot_row, axis=1)]
  transfers between devices with their start and end apart: 30 -> 35, of which waited for: 13 -> 19; matrix products, arithmetic and copies ran while one was open for 18% -> 15% of each run, Pallas kernels for 0% -> 0%
where the time goes in v4:
time: 209 us; the launch traced here: 207 us
  waiting for transfers between devices  64 us (31%)
  blocking collectives  48 us (23%)
  starting transfers between devices  36.9 us (18%)
  matrix products  35.5 us (17%)
  between operations  14.7 us (7%)
  other arithmetic  4.43 us (2%)
  local copies, waits for them, and re-layouts  3.81 us (2%)
    dot_general x11, matrix products, dot(): jnp.dot(a, b, precision=precision, preferred_element_type=jnp.float32)  35.5 us
    ppermute x9, waiting for transfers between devices, send_y(): lax.ppermute(array, 'row', y_shift(rows, by))  30.9 us
    all_to_all x2, blocking collectives, scatter_z(): lax.all_to_all(parts, 'row', 0, 0, axis_index_groups=z_groups(rows))  28.7 us
    all_gather x1, blocking collectives, on_device(): chosen = lax.all_gather(mine, 'col', axis=0, tiled=True)  19.2 us
    ppermute x14, starting transfers between devices, send(): return lax.ppermute(array, 'col', pairs)  14.8 us
    ppermute x4, waiting for transfers between devices, on_device(): known.append(lax.ppermute(value, 'col', pairs))  13.1 us
    ppermute x3, waiting for transfers between devices, scatter_y(): total = total + lax.ppermute(give, 'row', y_shift(rows, by))  8.19 us
    ppermute x9, starting transfers between devices, send_y(): lax.ppermute(array, 'row', y_shift(rows, by))  6.84 us
  transfers between devices with their start and end apart: 35, of which 19 were waited for; matrix products, arithmetic and copies ran while one was open for 15% of the time, Pallas kernels for 0%

profile of v4, /device:TPU:1, one launch (start us, length us, event | category | flops | bytes accessed | tf_op | source)
XLA Modules:
  0.0 207.3 jit_solution(1084527191194885862)
XLA Ops:
  6.5 1.2 copy-done
  7.8 5.7 %fusion.3 = f32[256,1024]{1,0:T(8,128)S(1)} fusion(f32[256,1024]{1,0:T(8,128)S(1)} %bitcast.92, f32[1,1024,1024]{2,1,0:T(8,128)} %param.12), kind=kOutput, calls=%fused_computation.4 | convolution fusion | flops 3221225472 | bytes 6291456 | tf_op jit(solution)/shard_map/dot_general | solution.py:13
  13.5 0.7 collective-permute-start
  14.2 4.6 %collective-permute-start.1 = (f32[32,1024]{1,0:T(8,128)S(1)}, f32[32,1024]{1,0:T(8,128)S(1)}, u32[]{:S(2)}, u32[]{:S(2)}) collective-permute-start(f32[32,1024]{1,0:T(8,128)S(1)} %get-tuple-element.47), channel_id=1, source_target_pairs={{4,2},{1,3},{0,7},{12,10},{9,11},{8,15},{20,18},{17,19},{16,23},{2... | collective-permute-start | bytes 393224 | tf_op jit(solution)/shard_map/ppermute | solution.py:75
  18.8 1.9 collective-permute-done.1
  20.7 2.8 %collective-permute-start.10 = (f32[32,1024]{1,0:T(8,128)S(1)}, f32[32,1024]{1,0:T(8,128)S(1)}, u32[]{:S(2)}, u32[]{:S(2)}) collective-permute-start(f32[32,1024]{1,0:T(8,128)S(1)} %get-tuple-element.45), channel_id=1, source_target_pairs={{8,0},{16,8},{24,16},{0,24},{40,32},{48,40},{56,48},{32,56},{72,64... | collective-permute-start | bytes 393224 | tf_op jit(solution)/shard_map/ppermute | solution.py:25
  23.9 0.7 collective-permute-start.12
  24.6 2.3 %collective-permute-done.10 = f32[32,1024]{1,0:T(8,128)S(1)} collective-permute-done((f32[32,1024]{1,0:T(8,128)S(1)}, f32[32,1024]{1,0:T(8,128)S(1)}, u32[]{:S(2)}, u32[]{:S(2)}) %collective-permute-start.10) | collective-permute-done | bytes 131104 | tf_op jit(solution)/shard_map/ppermute | solution.py:25
  26.9 2.1 %collective-permute-done.11 = f32[32,1024]{1,0:T(8,128)S(1)} collective-permute-done((f32[32,1024]{1,0:T(8,128)S(1)}, f32[32,1024]{1,0:T(8,128)S(1)}, u32[]{:S(2)}, u32[]{:S(2)}) %collective-permute-start.11) | collective-permute-done | bytes 131104 | tf_op jit(solution)/shard_map/ppermute | solution.py:25
  29.0 1.3 collective-permute-done.12
  30.4 0.9 pad_maximum_fusion
  32.0 2.0 fusion.6
  34.0 19.2 %all_gather.9 = f32[128,1024]{1,0:T(8,128)S(1)} all-gather(f32[16,1024]{1,0:T(8,128)S(1)} %fusion.6), channel_id=1, replica_groups=mesh['row'=32,'col'=8] {'col'}, dimensions={0}, use_global_device_ids=true | all-gather | bytes 589824 | tf_op jit(solution)/shard_map/all_gather | solution.py:98
  53.9 0.8 collective-permute-start.4
  54.7 4.6 %fusion.26 = f32[128,1024]{1,0:T(8,128)S(1)} fusion(f32[128,1024]{1,0:T(8,128)S(1)} %all_gather.9, f32[1024,1024]{1,0:T(8,128)} %param.7), kind=kOutput, calls=%fused_computation.60 | convolution fusion | flops 1610612736 | bytes 5242880 | tf_op jit(solution)/shard_map/dot_general | solution.py:13
  59.6 3.7 %collective-permute-done.4 = f32[32,1024]{1,0:T(8,128)S(1)} collective-permute-done((f32[32,1024]{1,0:T(8,128)S(1)}, f32[32,1024]{1,0:T(8,128)S(1)}, u32[]{:S(2)}, u32[]{:S(2)}) %collective-permute-start.4) | collective-permute-done | bytes 131104 | tf_op jit(solution)/shard_map/ppermute | solution.py:25
  63.5 0.8 pad_maximum_fusion.1
  64.6 0.8 dynamic-slice_bitcast_fusion.2
  65.6 1.3 collective-permute-start.7
  67.0 3.3 %collective-permute-done.5 = f32[8,4,1024]{2,1,0:T(4,128)} collective-permute-done((f32[8,4,1024]{2,1,0:T(4,128)}, f32[8,4,1024]{2,1,0:T(4,128)}, u32[]{:S(2)}, u32[]{:S(2)}) %collective-permute-start.5) | collective-permute-done | bytes 131104 | tf_op jit(solution)/shard_map/ppermute | solution.py:57
  70.3 0.7 collective-permute-done.6
  71.0 4.2 %collective-permute-done.7 = f32[8,4,1024]{2,1,0:T(4,128)} collective-permute-done((f32[8,4,1024]{2,1,0:T(4,128)}, f32[8,4,1024]{2,1,0:T(4,128)}, u32[]{:S(2)}, u32[]{:S(2)}) %collective-permute-start.7) | collective-permute-done | bytes 131104 | tf_op jit(solution)/shard_map/ppermute | solution.py:57
  75.2 1.1 fusion.9
  76.3 18.4 %all_to_all.15 = f32[8,4,1024]{2,1,0:T(4,128)S(1)} all-to-all(f32[8,4,1024]{2,1,0:T(4,128)S(1)} %fusion.9), channel_id=1, replica_groups={{0,32,64,96,128,160,192,224},{8,40,72,104,136,168,200,232},{16,48,80,11..., dimensions={0} | all-to-all | bytes 262144 | tf_op jit(solution)/shard_map/all_to_all | solution.py:48
  94.7 4.3 %fusion.1 = f32[4,1024]{1,0:T(4,128)S(1)} fusion(f32[1,1024,1024]{2,1,0:T(8,128)} %param.12, f32[4,1024]{1,0:T(4,128)S(1)} %copy-done.5, f32[4,1024]{1,0:T(4,128)S(1)} %reduce_sum.18), kind=kOutput, calls=%fused_computation.2 | convolution fusion | flops 50335744 | bytes 4243456 | tf_op jit(solution)/shard_map/dot_general | solution.py:13
  99.0 0.7 collective-permute-start.8
  99.7 0.7 collective-permute-start.9
  100.4 3.3 %select_subtract_fusion.1 = (f32[4,1024]{1,0:T(4,128)S(1)}, f32[4,1024]{1,0:T(4,128)S(1)}) fusion(f32[4,1024]{1,0:T(4,128)S(1)} %fusion.1, pred[]{:T(512)S(6)} %eq.40, f32[1024,1024]{1,0:T(8,128)} %all-gather.3.cloned.1.call-done, f32[4,1024]{1,0:T(4,128)S(1)} %collective-permute-done.8, f32[4,1024]{1,0:T(4,128)S(1)} %collective-permute-done.9, pred[]{:T(512)S(6)} %eq.80), kind=kOutput, calls=%fused_computation.51 | convolution fusion | flops 25182208 | bytes 4276226 | tf_op jit(solution)/shard_map/dot_general | solution.py:13
  103.7 0.7 collective-permute-start.13
  104.4 0.7 collective-permute-start.14
  105.0 0.7 collective-permute-start.15
  105.7 3.5 %fusion.17 = f32[4,1024]{1,0:T(4,128)S(1)} fusion(f32[1024,1024]{1,0:T(8,128)} %all-gather.3.cloned.1.call-done, f32[4,1024]{1,0:T(4,128)S(1)} %collective-permute-done.13, f32[4,1024]{1,0:T(4,128)S(1)} %collective-permute-done.14), kind=kOutput, calls=%fused_computation.49 | convolution fusion | flops 25169920 | bytes 4243456 | tf_op jit(solution)/shard_map/dot_general | solution.py:13
  109.2 0.7 collective-permute-start.16
  110.1 1.3 collective-permute-start.20
  111.5 0.8 collective-permute-start.17
  112.3 3.4 %fusion.27 = f32[4,1024]{1,0:T(4,128)S(1)} fusion(f32[4,1024]{1,0:T(4,128)S(1)} %collective-permute-done.16, f32[1024,1024]{1,0:T(8,128)} %all-gather.3.cloned.1.call-done), kind=kOutput, calls=%fused_computation.61 | convolution fusion | flops 25165824 | bytes 4227072 | tf_op jit(solution)/shard_map/dot_general | solution.py:13
  115.7 6.4 %collective-permute-done.18 = f32[4,32,1024]{2,1,0:T(8,128)S(1)} collective-permute-done((f32[4,32,1024]{2,1,0:T(8,128)S(1)}, f32[4,32,1024]{2,1,0:T(8,128)S(1)}, u32[]{:S(2)}, u32[]{:S(2)}) %collective-permute-start.18) | collective-permute-done | bytes 524320 | tf_op jit(solution)/shard_map/ppermute | solution.py:25
  122.0 0.7 collective-permute-done.19
  122.7 14.1 %collective-permute-done.20 = f32[4,32,1024]{2,1,0:T(8,128)S(1)} collective-permute-done((f32[4,32,1024]{2,1,0:T(8,128)S(1)}, f32[4,32,1024]{2,1,0:T(8,128)S(1)}, u32[]{:S(2)}, u32[]{:S(2)}) %collective-permute-start.20) | collective-permute-done | bytes 524320 | tf_op jit(solution)/shard_map/ppermute | solution.py:25
  136.8 1.3 collective-permute-start.21
  138.1 1.3 collective-permute-start.22
  139.4 1.3 collective-permute-start.23
  140.7 1.3 collective-permute-start.24
  142.5 7.5 %collective-permute-done.21 = f32[4,1024]{1,0:T(4,128)S(1)} collective-permute-done((f32[4,1024]{1,0:T(4,128)S(1)}, f32[4,1024]{1,0:T(4,128)S(1)}, u32[]{:S(2)}, u32[]{:S(2)}) %collective-permute-start.21) | collective-permute-done | bytes 16416 | tf_op jit(solution)/shard_map/ppermute | solution.py:141
  149.9 3.6 %collective-permute-done.22 = f32[4,1024]{1,0:T(4,128)S(1)} collective-permute-done((f32[4,1024]{1,0:T(4,128)S(1)}, f32[4,1024]{1,0:T(4,128)S(1)}, u32[]{:S(2)}, u32[]{:S(2)}) %collective-permute-start.22) | collective-permute-done | bytes 16416 | tf_op jit(solution)/shard_map/ppermute | solution.py:141
  153.5 0.7 collective-permute-done.23
  154.3 1.3 collective-permute-done.24
  155.5 0.6 maximum_bitcast_fusion
  156.2 3.3 %all-to-all-start.1 = ((f32[8,4,4,128]{3,1,2,0:T(4,128)}), f32[8,4,4,128]{3,1,2,0:T(4,128)S(1)}, u32[]{:S(2)}, u32[]{:S(2)}) async-start(f32[8,4,4,128]{3,1,2,0:T(4,128)} %maximum_bitcast_fusion), calls=%async_computation.1 | async-start | bytes 131072 | tf_op jit(solution)/shard_map/all_to_all | solution.py:145
  159.5 1.1 bitcast_dynamic-update-slice_fusion
  160.6 6.1 %all-to-all-done.1 = f32[8,4,4,128]{3,1,2,0:T(4,128)S(1)} async-done(((f32[8,4,4,128]{3,1,2,0:T(4,128)}), f32[8,4,4,128]{3,1,2,0:T(4,128)S(1)}, u32[]{:S(2)}, u32[]{:S(2)}) %all-to-all-start.1) | async-done | bytes 65568 | tf_op jit(solution)/shard_map/all_to_all | solution.py:145
  166.8 0.7 fusion.10
  167.5 10.4 %all_to_all.16 = f32[8,4,1024]{2,1,0:T(4,128)S(1)} all-to-all(f32[8,4,1024]{2,1,0:T(4,128)S(1)} %fusion.10), channel_id=1, replica_groups={{0,32,64,96,128,160,192,224},{8,40,72,104,136,168,200,232},{16,48,80,11..., dimensions={0} | all-to-all | bytes 262144 | tf_op jit(solution)/shard_map/all_to_all | solution.py:48
  177.9 0.7 collective-permute-start.25
  178.6 0.9 collective-permute-start.26
  179.6 3.3 %select_subtract_fusion = (f32[4,1024]{1,0:T(4,128)S(1)}, f32[4,1024]{1,0:T(4,128)S(1)}) fusion(f32[4,1024]{1,0:T(4,128)S(1)} %sub.54, pred[]{:T(512)S(6)} %eq.82, f32[1024,1024]{1,0:T(8,128)} %all-gather.5.cloned.1.call-done, f32[4,1024]{1,0:T(4,128)S(1)} %collective-permute-done.25, f32[4,1024]{1,0:T(4,128)S(1)} %collective-permute-done.26, pred[]{:T(512)S(6)} %eq.86), kind=kOutput, calls=%fused_computation.43 | convolution fusion | flops 25182208 | bytes 4276226 | tf_op jit(solution)/shard_map/dot_general | solution.py:13
  182.9 1.3 collective-permute-start.27
  184.2 0.7 collective-permute-start.28
  184.9 1.6 collective-permute-start.29
  186.4 3.6 %collective-permute-done.27 = f32[4,1024]{1,0:T(4,128)S(1)} collective-permute-done((f32[4,1024]{1,0:T(4,128)S(1)}, f32[4,1024]{1,0:T(4,128)S(1)}, u32[]{:S(2)}, u32[]{:S(2)}) %collective-permute-start.27) | collective-permute-done | bytes 16416 | tf_op jit(solution)/shard_map/ppermute | solution.py:116
  190.0 3.3 %fusion.12 = f32[4,1024]{1,0:T(4,128)S(1)} fusion(f32[1024,1024]{1,0:T(8,128)} %all-gather.5.cloned.1.call-done, f32[4,1024]{1,0:T(4,128)S(1)} %collective-permute-done.27, f32[4,1024]{1,0:T(4,128)S(1)} %collective-permute-done.28), kind=kOutput, calls=%fused_computation.41 | convolution fusion | flops 25169920 | bytes 4243456 | tf_op jit(solution)/shard_map/dot_general | solution.py:13
  193.4 4.3 %collective-permute-start.30 = (f32[4,1024]{1,0:T(4,128)S(1)}, f32[4,1024]{1,0:T(4,128)S(1)}, u32[]{:S(2)}, u32[]{:S(2)}) collective-permute-start(f32[4,1024]{1,0:T(4,128)S(1)} %subtract_subtract_fusion.1), channel_id=1, source_target_pairs={{1,0},{9,8},{17,16},{25,24},{33,32},{41,40},{49,48},{57,56},{65,64... | collective-permute-start | bytes 49160 | tf_op jit(solution)/shard_map/ppermute | solution.py:116
  197.7 0.7 collective-permute-start.31
  198.5 1.4 fusion.28
  (65 shorter events, 3.7 us)
Async XLA Ops:
  6.5 1.2 copy-start
  6.5 93.8 %all-gather.3.cloned.1.call-start = ((), (), s32[]{:S(2)}) async-start(), calls=%async_computation.3 | async-start | bytes 4718592 | tf_op jit(solution)/shard_map/all_gather | solution.py:82
  7.8 24.2 %copy-start.6 = (s32[1024]{0:T(1024)S(1)}, s32[1024]{0:T(1024)}, u32[]{:S(2)}) copy-start(s32[1024]{0:T(1024)} %param.9) | copy-start | bytes 12292
  7.8 24.2 %copy-start.7 = (f32[16,1536]{1,0:T(8,128)S(1)}, f32[16,1536]{1,0:T(8,128)}, u32[]{:S(2)}) copy-start(f32[16,1536]{1,0:T(8,128)} %param.8) | copy-start | bytes 294916
  13.5 5.3 %collective-permute-start = (f32[32,1024]{1,0:T(8,128)S(1)}, f32[32,1024]{1,0:T(8,128)S(1)}, u32[]{:S(2)}, u32[]{:S(2)}) collective-permute-start(f32[32,1024]{1,0:T(8,128)S(1)} %get-tuple-element.48), channel_id=1, source_target_pairs={{5,7},{4,3},{0,6},{13,15},{12,11},{8,14},{21,23},{20,19},{16,22},{... | collective-permute-start | bytes 393224 | tf_op jit(solution)/shard_map/ppermute | solution.py:74
  14.2 6.5 %collective-permute-start.1 = (f32[32,1024]{1,0:T(8,128)S(1)}, f32[32,1024]{1,0:T(8,128)S(1)}, u32[]{:S(2)}, u32[]{:S(2)}) collective-permute-start(f32[32,1024]{1,0:T(8,128)S(1)} %get-tuple-element.47), channel_id=1, source_target_pairs={{4,2},{1,3},{0,7},{12,10},{9,11},{8,15},{20,18},{17,19},{16,23},{2... | collective-permute-start | bytes 393224 | tf_op jit(solution)/shard_map/ppermute | solution.py:75
  20.7 6.1 %collective-permute-start.10 = (f32[32,1024]{1,0:T(8,128)S(1)}, f32[32,1024]{1,0:T(8,128)S(1)}, u32[]{:S(2)}, u32[]{:S(2)}) collective-permute-start(f32[32,1024]{1,0:T(8,128)S(1)} %get-tuple-element.45), channel_id=1, source_target_pairs={{8,0},{16,8},{24,16},{0,24},{40,32},{48,40},{56,48},{32,56},{72,64... | collective-permute-start | bytes 393224 | tf_op jit(solution)/shard_map/ppermute | solution.py:25
  23.6 5.4 %collective-permute-start.11 = (f32[32,1024]{1,0:T(8,128)S(1)}, f32[32,1024]{1,0:T(8,128)S(1)}, u32[]{:S(2)}, u32[]{:S(2)}) collective-permute-start(f32[32,1024]{1,0:T(8,128)S(1)} %get-tuple-element.45), channel_id=1, source_target_pairs={{16,0},{24,8},{0,16},{8,24},{48,32},{56,40},{32,48},{40,56},{80,64... | collective-permute-start | bytes 393224 | tf_op jit(solution)/shard_map/ppermute | solution.py:25
  23.9 6.4 %collective-permute-start.12 = (f32[32,1024]{1,0:T(8,128)S(1)}, f32[32,1024]{1,0:T(8,128)S(1)}, u32[]{:S(2)}, u32[]{:S(2)}) collective-permute-start(f32[32,1024]{1,0:T(8,128)S(1)} %get-tuple-element.45), channel_id=1, source_target_pairs={{24,0},{0,8},{8,16},{16,24},{56,32},{32,40},{40,48},{48,56},{88,64... | collective-permute-start | bytes 393224 | tf_op jit(solution)/shard_map/ppermute | solution.py:25
  31.2 148.3 %all-gather.5.cloned.1.call-start = ((), (), s32[]{:S(2)}) async-start(), calls=%async_computation.4 | async-start | bytes 4718592 | tf_op jit(solution)/shard_map/all_gather | solution.py:82
  53.2 6.1 %collective-permute-start.2 = (f32[32,1024]{1,0:T(8,128)S(1)}, f32[32,1024]{1,0:T(8,128)S(1)}, u32[]{:S(2)}, u32[]{:S(2)}) collective-permute-start(f32[32,1024]{1,0:T(8,128)S(1)} %get-tuple-element.40), channel_id=1, source_target_pairs={{8,0},{16,8},{24,16},{0,24},{40,32},{48,40},{56,48},{32,56},{72,64... | collective-permute-start | bytes 393224 | tf_op jit(solution)/shard_map/ppermute | solution.py:25
  53.5 6.1 %collective-permute-start.3 = (f32[32,1024]{1,0:T(8,128)S(1)}, f32[32,1024]{1,0:T(8,128)S(1)}, u32[]{:S(2)}, u32[]{:S(2)}) collective-permute-start(f32[32,1024]{1,0:T(8,128)S(1)} %get-tuple-element.40), channel_id=1, source_target_pairs={{16,0},{24,8},{0,16},{8,24},{48,32},{56,40},{32,48},{40,56},{80,64... | collective-permute-start | bytes 393224 | tf_op jit(solution)/shard_map/ppermute | solution.py:25
  53.9 9.5 %collective-permute-start.4 = (f32[32,1024]{1,0:T(8,128)S(1)}, f32[32,1024]{1,0:T(8,128)S(1)}, u32[]{:S(2)}, u32[]{:S(2)}) collective-permute-start(f32[32,1024]{1,0:T(8,128)S(1)} %get-tuple-element.40), channel_id=1, source_target_pairs={{24,0},{0,8},{8,16},{16,24},{56,32},{32,40},{40,48},{48,56},{88,64... | collective-permute-start | bytes 393224 | tf_op jit(solution)/shard_map/ppermute | solution.py:25
  63.5 31.3 %copy-start.5 = (f32[4,1024]{1,0:T(4,128)S(1)}, f32[4,1024]{1,0:T(4,128)}, u32[]{:S(2)}) copy-start(f32[4,1024]{1,0:T(4,128)} %param.13) | copy-start | bytes 49156
  65.3 5.0 %collective-permute-start.5 = (f32[8,4,1024]{2,1,0:T(4,128)}, f32[8,4,1024]{2,1,0:T(4,128)}, u32[]{:S(2)}, u32[]{:S(2)}) collective-permute-start(f32[8,4,1024]{2,1,0:T(4,128)} %get-tuple-element.49), channel_id=1, source_target_pairs={{8,0},{16,8},{24,16},{0,24},{40,32},{48,40},{56,48},{32,56},{72,64... | collective-permute-start | bytes 393224 | tf_op jit(solution)/shard_map/ppermute | solution.py:57
  65.3 5.7 %collective-permute-start.6 = (f32[8,4,1024]{2,1,0:T(4,128)}, f32[8,4,1024]{2,1,0:T(4,128)}, u32[]{:S(2)}, u32[]{:S(2)}) collective-permute-start(f32[8,4,1024]{2,1,0:T(4,128)} %get-tuple-element.51), channel_id=1, source_target_pairs={{16,0},{24,8},{0,16},{8,24},{48,32},{56,40},{32,48},{40,56},{80,64... | collective-permute-start | bytes 393224 | tf_op jit(solution)/shard_map/ppermute | solution.py:57
  65.6 9.7 %collective-permute-start.7 = (f32[8,4,1024]{2,1,0:T(4,128)}, f32[8,4,1024]{2,1,0:T(4,128)}, u32[]{:S(2)}, u32[]{:S(2)}) collective-permute-start(f32[8,4,1024]{2,1,0:T(4,128)} %get-tuple-element.50), channel_id=1, source_target_pairs={{24,0},{0,8},{8,16},{16,24},{56,32},{32,40},{40,48},{48,56},{88,64... | collective-permute-start | bytes 393224 | tf_op jit(solution)/shard_map/ppermute | solution.py:57
  67.0 43.1 %copy-start.2 = (f32[4,32,1024]{2,1,0:T(8,128)}, f32[4,32,1024]{2,1,0:T(8,128)S(1)}, u32[]{:S(2)}) copy-start(f32[4,32,1024]{2,1,0:T(8,128)S(1)} %fusion.7) | copy-start | bytes 1572868
  99.0 1.3 collective-permute-start.8
  99.7 0.7 collective-permute-start.9
  103.7 2.0 collective-permute-start.13
  104.4 1.4 collective-permute-start.14
  105.0 4.2 %collective-permute-start.15 = (f32[4,1024]{1,0:T(4,128)S(1)}, f32[4,1024]{1,0:T(4,128)S(1)}, u32[]{:S(2)}, u32[]{:S(2)}) collective-permute-start(f32[4,1024]{1,0:T(4,128)S(1)} %get-tuple-element.61), channel_id=1, source_target_pairs={{7,5},{3,4},{15,13},{11,12},{23,21},{19,20},{31,29},{27,28},{39,37... | collective-permute-start | bytes 49160 | tf_op jit(solution)/shard_map/ppermute | solution.py:116
  109.2 3.0 %collective-permute-start.16 = (f32[4,1024]{1,0:T(4,128)S(1)}, f32[4,1024]{1,0:T(4,128)S(1)}, u32[]{:S(2)}, u32[]{:S(2)}) collective-permute-start(f32[4,1024]{1,0:T(4,128)S(1)} %subtract_subtract_fusion.3), channel_id=1, source_target_pairs={{5,4},{13,12},{21,20},{29,28},{37,36},{45,44},{53,52},{61,60},{69,... | collective-permute-start | bytes 49160 | tf_op jit(solution)/shard_map/ppermute | solution.py:116
  109.9 12.1 %collective-permute-start.18 = (f32[4,32,1024]{2,1,0:T(8,128)S(1)}, f32[4,32,1024]{2,1,0:T(8,128)S(1)}, u32[]{:S(2)}, u32[]{:S(2)}) collective-permute-start(f32[4,32,1024]{2,1,0:T(8,128)S(1)} %fusion.7), channel_id=1, source_target_pairs={{8,0},{16,8},{24,16},{0,24},{40,32},{48,40},{56,48},{32,56},{72,64... | collective-permute-start | bytes 1572872 | tf_op jit(solution)/shard_map/ppermute | solution.py:25
  110.0 12.7 %collective-permute-start.19 = (f32[4,32,1024]{2,1,0:T(8,128)S(1)}, f32[4,32,1024]{2,1,0:T(8,128)S(1)}, u32[]{:S(2)}, u32[]{:S(2)}) collective-permute-start(f32[4,32,1024]{2,1,0:T(8,128)S(1)} %fusion.7), channel_id=1, source_target_pairs={{16,0},{24,8},{0,16},{8,24},{48,32},{56,40},{32,48},{40,56},{80,64... | collective-permute-start | bytes 1572872 | tf_op jit(solution)/shard_map/ppermute | solution.py:25
  110.1 26.7 %collective-permute-start.20 = (f32[4,32,1024]{2,1,0:T(8,128)S(1)}, f32[4,32,1024]{2,1,0:T(8,128)S(1)}, u32[]{:S(2)}, u32[]{:S(2)}) collective-permute-start(f32[4,32,1024]{2,1,0:T(8,128)S(1)} %fusion.7), channel_id=1, source_target_pairs={{24,0},{0,8},{8,16},{16,24},{56,32},{32,40},{40,48},{48,56},{88,64... | collective-permute-start | bytes 1572872 | tf_op jit(solution)/shard_map/ppermute | solution.py:25
  111.5 30.8 %copy-start.3 = (f32[4,32,1024]{2,1,0:T(8,128)S(1)}, f32[4,32,1024]{2,1,0:T(8,128)}, u32[]{:S(2)}) copy-start(f32[4,32,1024]{2,1,0:T(8,128)} %copy-done.2) | copy-start | bytes 1572868
  111.5 4.2 %collective-permute-start.17 = (f32[4,1024]{1,0:T(4,128)S(1)}, f32[4,1024]{1,0:T(4,128)S(1)}, u32[]{:S(2)}, u32[]{:S(2)}) collective-permute-start(f32[4,1024]{1,0:T(4,128)S(1)} %fusion.17), channel_id=1, source_target_pairs={{2,4},{10,12},{18,20},{26,28},{34,36},{42,44},{50,52},{58,60},{66,... | collective-permute-start | bytes 49160 | tf_op jit(solution)/shard_map/ppermute | solution.py:116
  136.8 5.7 %copy-start.4 = (f32[4,32,1024]{2,1,0:T(8,128)}, f32[4,32,1024]{2,1,0:T(8,128)S(1)}, u32[]{:S(2)}) copy-start(f32[4,32,1024]{2,1,0:T(8,128)S(1)} %collective-permute-done.20) | copy-start | bytes 1572868
  136.8 13.1 %collective-permute-start.21 = (f32[4,1024]{1,0:T(4,128)S(1)}, f32[4,1024]{1,0:T(4,128)S(1)}, u32[]{:S(2)}, u32[]{:S(2)}) collective-permute-start(f32[4,1024]{1,0:T(4,128)S(1)} %subtract_subtract_fusion.2), channel_id=1, source_target_pairs={{4,0},{5,1},{6,2},{7,3},{12,8},{13,9},{14,10},{15,11},{20,16},{21,... | collective-permute-start | bytes 49160 | tf_op jit(solution)/shard_map/ppermute | solution.py:141
  138.1 15.4 %collective-permute-start.22 = (f32[4,1024]{1,0:T(4,128)S(1)}, f32[4,1024]{1,0:T(4,128)S(1)}, u32[]{:S(2)}, u32[]{:S(2)}) collective-permute-start(f32[4,1024]{1,0:T(4,128)S(1)} %subtract_subtract_fusion.2), channel_id=1, source_target_pairs={{5,0},{6,1},{7,2},{4,3},{13,8},{14,9},{15,10},{12,11},{21,16},{22,... | collective-permute-start | bytes 49160 | tf_op jit(solution)/shard_map/ppermute | solution.py:141
  139.4 14.8 %collective-permute-start.23 = (f32[4,1024]{1,0:T(4,128)S(1)}, f32[4,1024]{1,0:T(4,128)S(1)}, u32[]{:S(2)}, u32[]{:S(2)}) collective-permute-start(f32[4,1024]{1,0:T(4,128)S(1)} %subtract_subtract_fusion.2), channel_id=1, source_target_pairs={{6,0},{7,1},{4,2},{5,3},{14,8},{15,9},{12,10},{13,11},{22,16},{23,... | collective-permute-start | bytes 49160 | tf_op jit(solution)/shard_map/ppermute | solution.py:141
  140.7 14.8 %collective-permute-start.24 = (f32[4,1024]{1,0:T(4,128)S(1)}, f32[4,1024]{1,0:T(4,128)S(1)}, u32[]{:S(2)}, u32[]{:S(2)}) collective-permute-start(f32[4,1024]{1,0:T(4,128)S(1)} %subtract_subtract_fusion.2), channel_id=1, source_target_pairs={{7,0},{4,1},{5,2},{6,3},{15,8},{12,9},{13,10},{14,11},{23,16},{20,... | collective-permute-start | bytes 49160 | tf_op jit(solution)/shard_map/ppermute | solution.py:141
  156.2 10.6 %all-to-all-start.1 = ((f32[8,4,4,128]{3,1,2,0:T(4,128)}), f32[8,4,4,128]{3,1,2,0:T(4,128)S(1)}, u32[]{:S(2)}, u32[]{:S(2)}) async-start(f32[8,4,4,128]{3,1,2,0:T(4,128)} %maximum_bitcast_fusion), calls=%async_computation.1 | async-start | bytes 131072 | tf_op jit(solution)/shard_map/all_to_all | solution.py:145
  177.9 1.6 collective-permute-start.25
  178.6 0.9 collective-permute-start.26
  182.9 7.2 %collective-permute-start.27 = (f32[4,1024]{1,0:T(4,128)S(1)}, f32[4,1024]{1,0:T(4,128)S(1)}, u32[]{:S(2)}, u32[]{:S(2)}) collective-permute-start(f32[4,1024]{1,0:T(4,128)S(1)} %get-tuple-element.62), channel_id=1, source_target_pairs={{2,1},{10,9},{18,17},{26,25},{34,33},{42,41},{50,49},{58,57},{66,6... | collective-permute-start | bytes 49160 | tf_op jit(solution)/shard_map/ppermute | solution.py:116
  184.2 5.9 %collective-permute-start.28 = (f32[4,1024]{1,0:T(4,128)S(1)}, f32[4,1024]{1,0:T(4,128)S(1)}, u32[]{:S(2)}, u32[]{:S(2)}) collective-permute-start(f32[4,1024]{1,0:T(4,128)S(1)} %get-tuple-element.62), channel_id=1, source_target_pairs={{2,6},{10,14},{18,22},{26,30},{34,38},{42,46},{50,54},{58,62},{66,... | collective-permute-start | bytes 49160 | tf_op jit(solution)/shard_map/ppermute | solution.py:116
  184.8 13.7 %copy-start.1 = (f32[1024,1024]{1,0:T(8,128)S(1)}, f32[1024,1024]{1,0:T(8,128)}, u32[]{:S(2)}) copy-start(f32[1024,1024]{1,0:T(8,128)} %all-gather.5.cloned.1.call-done) | copy-start | bytes 12582916
  184.9 8.5 %collective-permute-start.29 = (f32[4,1024]{1,0:T(4,128)S(1)}, f32[4,1024]{1,0:T(4,128)S(1)}, u32[]{:S(2)}, u32[]{:S(2)}) collective-permute-start(f32[4,1024]{1,0:T(4,128)S(1)} %get-tuple-element.63), channel_id=1, source_target_pairs={{3,1},{7,0},{11,9},{15,8},{19,17},{23,16},{27,25},{31,24},{35,33},... | collective-permute-start | bytes 49160 | tf_op jit(solution)/shard_map/ppermute | solution.py:116
  193.4 5.2 %collective-permute-start.30 = (f32[4,1024]{1,0:T(4,128)S(1)}, f32[4,1024]{1,0:T(4,128)S(1)}, u32[]{:S(2)}, u32[]{:S(2)}) collective-permute-start(f32[4,1024]{1,0:T(4,128)S(1)} %subtract_subtract_fusion.1), channel_id=1, source_target_pairs={{1,0},{9,8},{17,16},{25,24},{33,32},{41,40},{49,48},{57,56},{65,64... | collective-permute-start | bytes 49160 | tf_op jit(solution)/shard_map/ppermute | solution.py:116
  197.7 2.2 %collective-permute-start.31 = (f32[4,1024]{1,0:T(4,128)S(1)}, f32[4,1024]{1,0:T(4,128)S(1)}, u32[]{:S(2)}, u32[]{:S(2)}) collective-permute-start(f32[4,1024]{1,0:T(4,128)S(1)} %fusion.12), channel_id=1, source_target_pairs={{6,0},{14,8},{22,16},{30,24},{38,32},{46,40},{54,48},{62,56},{70,6... | collective-permute-start | bytes 49160 | tf_op jit(solution)/shard_map/ppermute | solution.py:116
Sparse Core Ops, SparseCore 0:
  31.4 63.0 all-gather.2
  96.3 53.7 all-gather.4

commit v5 on v4

--- a/solution.py
+++ b/solution.py
@@ -103,10 +103,10 @@
     total = scatter_y(term, rows)
     twice = jnp.concatenate([scaled[HALF:], scaled[HALF:-1]], axis=0)
     far = lax.dynamic_slice_in_dim(twice, column % HALF, HALF, 0)
-    total, far = lax.optimization_barrier((total, far))
+    far, lower = lax.optimization_barrier((far, lower))
     far = send_y(far, rows)
     total = scatter_z(total, rows)
-    value = dot(rhs - total, diag)
+    value = dot(rhs - total, diag, lax.Precision.HIGH)
 
     def solve_half(value, low, near):
         a, b, c, d = low, low + 1, low + 2, low + 3
@@ -121,15 +121,16 @@
         got = send(value, [(d, c)]) + send(value, [(d, first)])
         term = times(jnp.where(column == d, value, got))
         value = value - jnp.where(column == c, term, 0.0)
-        aside = send(term, [(d, b), (first, a)])
+        aside = send(term, [(d, b)])
+        early = send(term, [(first, a)])
         got = send(value, [(c, b)]) + send(value, [(c, second)])
         term = times(got)
         last = send(term, [(second, a)])
         term, aside = lax.optimization_barrier((term, aside))
         value = value - jnp.where(column == b, term, 0.0) - aside
         term = times(send(value, [(b, a)]))
-        term, last = lax.optimization_barrier((term, last))
-        return value - term - last
+        term, last, early = lax.optimization_barrier((term, last, early))
+        return value - term - (last + early)
 
     value = solve_half(value, HALF, upper_near)
     value, far = lax.optimization_barrier((value, far))

time: 209 us -> 206 us (0.986)
    ppermute x14 -> x16, starting transfers between devices: 14.8 us -> 12.9 us  [send(): return lax.ppermute(array, 'col', pairs)]
  transfers between devices with their start and end apart: 35 -> 37, of which waited for: 19 -> 18; matrix products, arithmetic and copies ran while one was open for 15% -> 15% of each run, Pallas kernels for 0% -> 0%
where the time goes in v5:
time: 206 us; the launch traced here: 203 us
  waiting for transfers between devices  62.7 us (30%)
  blocking collectives  48.1 us (23%)
  starting transfers between devices  35.2 us (17%)
  matrix products  34.4 us (17%)
  between operations  14.7 us (7%)
  other arithmetic  5.16 us (3%)
  local copies, waits for them, and re-layouts  3.06 us (1%)
    dot_general x11, matrix products, dot(): jnp.dot(a, b, precision=precision, preferred_element_type=jnp.float32)  34.4 us
    ppermute x9, waiting for transfers between devices, send_y(): lax.ppermute(array, 'row', y_shift(rows, by))  30.3 us
    all_to_all x2, blocking collectives, scatter_z(): lax.all_to_all(parts, 'row', 0, 0, axis_index_groups=z_groups(rows))  28.8 us
    all_gather x1, blocking collectives, on_device(): chosen = lax.all_gather(mine, 'col', axis=0, tiled=True)  19.2 us
    ppermute x16, starting transfers between devices, send(): return lax.ppermute(array, 'col', pairs)  12.9 us
    ppermute x4, waiting for transfers between devices, on_device(): known.append(lax.ppermute(value, 'col', pairs))  12 us
    ppermute x3, waiting for transfers between devices, scatter_y(): total = total + lax.ppermute(give, 'row', y_shift(rows, by))  8.24 us
    ppermute x9, starting transfers between devices, send_y(): lax.ppermute(array, 'row', y_shift(rows, by))  6.77 us
  transfers between devices with their start and end apart: 37, of which 18 were waited for; matrix products, arithmetic and copies ran while one was open for 15% of the time, Pallas kernels for 0%

profile of v5, /device:TPU:1, one launch (start us, length us, event | category | flops | bytes accessed | tf_op | source)
XLA Modules:
  0.0 203.3 jit_solution(769291052022316570)
XLA Ops:
  6.5 1.2 copy-done
  7.8 5.7 %fusion.3 = f32[256,1024]{1,0:T(8,128)S(1)} fusion(f32[256,1024]{1,0:T(8,128)S(1)} %bitcast.92, f32[1,1024,1024]{2,1,0:T(8,128)} %param.12), kind=kOutput, calls=%fused_computation.4 | convolution fusion | flops 3221225472 | bytes 6291456 | tf_op jit(solution)/shard_map/dot_general | solution.py:13
  13.5 0.7 collective-permute-start
  14.2 4.6 %collective-permute-start.1 = (f32[32,1024]{1,0:T(8,128)S(1)}, f32[32,1024]{1,0:T(8,128)S(1)}, u32[]{:S(2)}, u32[]{:S(2)}) collective-permute-start(f32[32,1024]{1,0:T(8,128)S(1)} %get-tuple-element.49), channel_id=1, source_target_pairs={{4,2},{1,3},{0,7},{12,10},{9,11},{8,15},{20,18},{17,19},{16,23},{2... | collective-permute-start | bytes 393224 | tf_op jit(solution)/shard_map/ppermute | solution.py:75
  18.8 1.9 collective-permute-done.1
  20.7 0.7 bitcast_select_fusion
  21.4 2.7 %collective-permute-start.10 = (f32[32,1024]{1,0:T(8,128)S(1)}, f32[32,1024]{1,0:T(8,128)S(1)}, u32[]{:S(2)}, u32[]{:S(2)}) collective-permute-start(f32[32,1024]{1,0:T(8,128)S(1)} %get-tuple-element.47), channel_id=1, source_target_pairs={{8,0},{16,8},{24,16},{0,24},{40,32},{48,40},{56,48},{32,56},{72,64... | collective-permute-start | bytes 393224 | tf_op jit(solution)/shard_map/ppermute | solution.py:25
  24.5 0.7 collective-permute-start.12
  25.2 2.3 %collective-permute-done.10 = f32[32,1024]{1,0:T(8,128)S(1)} collective-permute-done((f32[32,1024]{1,0:T(8,128)S(1)}, f32[32,1024]{1,0:T(8,128)S(1)}, u32[]{:S(2)}, u32[]{:S(2)}) %collective-permute-start.10) | collective-permute-done | bytes 131104 | tf_op jit(solution)/shard_map/ppermute | solution.py:25
  27.5 2.1 %collective-permute-done.11 = f32[32,1024]{1,0:T(8,128)S(1)} collective-permute-done((f32[32,1024]{1,0:T(8,128)S(1)}, f32[32,1024]{1,0:T(8,128)S(1)}, u32[]{:S(2)}, u32[]{:S(2)}) %collective-permute-start.11) | collective-permute-done | bytes 131104 | tf_op jit(solution)/shard_map/ppermute | solution.py:25
  29.6 1.3 collective-permute-done.12
  31.0 0.9 pad_maximum_fusion
  32.6 2.0 fusion.6
  34.6 19.2 %all_gather.9 = f32[128,1024]{1,0:T(8,128)S(1)} all-gather(f32[16,1024]{1,0:T(8,128)S(1)} %fusion.6), channel_id=1, replica_groups=mesh['row'=32,'col'=8] {'col'}, dimensions={0}, use_global_device_ids=true | all-gather | bytes 589824 | tf_op jit(solution)/shard_map/all_gather | solution.py:98
  54.5 0.8 collective-permute-start.4
  55.3 4.6 %fusion.26 = f32[128,1024]{1,0:T(8,128)S(1)} fusion(f32[128,1024]{1,0:T(8,128)S(1)} %all_gather.9, f32[1024,1024]{1,0:T(8,128)} %param.7), kind=kOutput, calls=%fused_computation.60 | convolution fusion | flops 1610612736 | bytes 5242880 | tf_op jit(solution)/shard_map/dot_general | solution.py:13
  60.6 3.6 %collective-permute-done.4 = f32[32,1024]{1,0:T(8,128)} collective-permute-done((f32[32,1024]{1,0:T(8,128)}, f32[32,1024]{1,0:T(8,128)}, u32[]{:S(2)}, u32[]{:S(2)}) %collective-permute-start.4) | collective-permute-done | bytes 131104 | tf_op jit(solution)/shard_map/ppermute | solution.py:25
  64.2 1.2 select_bitcast_fusion.3
  65.4 0.9 fusion.7
  67.0 1.1 collective-permute-start.7
  68.1 3.2 %collective-permute-done.5 = f32[8,4,1024]{2,1,0:T(4,128)S(1)} collective-permute-done((f32[8,4,1024]{2,1,0:T(4,128)S(1)}, f32[8,4,1024]{2,1,0:T(4,128)S(1)}, u32[]{:S(2)}, u32[]{:S(2)}) %collective-permute-start.5) | collective-permute-done | bytes 131104 | tf_op jit(solution)/shard_map/ppermute | solution.py:57
  71.3 0.8 collective-permute-done.6
  72.1 4.2 %collective-permute-done.7 = f32[8,4,1024]{2,1,0:T(4,128)S(1)} collective-permute-done((f32[8,4,1024]{2,1,0:T(4,128)S(1)}, f32[8,4,1024]{2,1,0:T(4,128)S(1)}, u32[]{:S(2)}, u32[]{:S(2)}) %collective-permute-start.7) | collective-permute-done | bytes 131104 | tf_op jit(solution)/shard_map/ppermute | solution.py:57
  76.4 18.4 %all_to_all.15 = f32[8,4,1024]{2,1,0:T(4,128)S(1)} all-to-all(f32[8,4,1024]{2,1,0:T(4,128)S(1)} %fusion.9), channel_id=1, replica_groups={{0,32,64,96,128,160,192,224},{8,40,72,104,136,168,200,232},{16,48,80,11..., dimensions={0} | all-to-all | bytes 262144 | tf_op jit(solution)/shard_map/all_to_all | solution.py:48
  94.9 3.3 %fusion.1 = f32[4,1024]{1,0:T(4,128)S(1)} fusion(f32[1,1024,1024]{2,1,0:T(8,128)} %param.12, f32[4,1024]{1,0:T(4,128)S(1)} %copy-done.5, f32[4,1024]{1,0:T(4,128)S(1)} %reduce_sum.18), kind=kOutput, calls=%fused_computation.2 | convolution fusion | flops 25169920 | bytes 4243456 | tf_op jit(solution)/shard_map/dot_general | solution.py:13
  98.2 0.7 collective-permute-start.8
  98.9 0.7 collective-permute-start.9
  99.6 3.3 %select_subtract_fusion.1 = (f32[4,1024]{1,0:T(4,128)S(1)}, f32[4,1024]{1,0:T(4,128)S(1)}) fusion(f32[4,1024]{1,0:T(4,128)S(1)} %fusion.1, pred[]{:T(512)S(6)} %eq.40, f32[1024,1024]{1,0:T(8,128)} %all-gather.3.cloned.1.call-done, f32[4,1024]{1,0:T(4,128)S(1)} %collective-permute-done.8, f32[4,1024]{1,0:T(4,128)S(1)} %collective-permute-done.9, pred[]{:T(512)S(6)} %eq.80), kind=kOutput, calls=%fused_computation.51 | convolution fusion | flops 25182208 | bytes 4276226 | tf_op jit(solution)/shard_map/dot_general | solution.py:13
  103.6 0.7 collective-permute-start.14
  104.3 0.7 collective-permute-start.15
  105.0 3.3 %fusion.17 = f32[4,1024]{1,0:T(4,128)S(1)} fusion(f32[1024,1024]{1,0:T(8,128)} %all-gather.3.cloned.1.call-done, f32[4,1024]{1,0:T(4,128)S(1)} %collective-permute-done.13, f32[4,1024]{1,0:T(4,128)S(1)} %collective-permute-done.14), kind=kOutput, calls=%fused_computation.49 | convolution fusion | flops 25169920 | bytes 4243456 | tf_op jit(solution)/shard_map/dot_general | solution.py:13
  108.3 0.7 collective-permute-start.16
  109.2 1.3 collective-permute-start.21
  110.5 0.8 collective-permute-start.18
  111.3 0.7 collective-permute-start.17
  112.0 3.4 %fusion.27 = f32[4,1024]{1,0:T(4,128)S(1)} fusion(f32[4,1024]{1,0:T(4,128)S(1)} %collective-permute-done.16, f32[1024,1024]{1,0:T(8,128)} %all-gather.3.cloned.1.call-done), kind=kOutput, calls=%fused_computation.61 | convolution fusion | flops 25165824 | bytes 4227072 | tf_op jit(solution)/shard_map/dot_general | solution.py:13
  115.4 5.5 %collective-permute-done.19 = f32[4,32,1024]{2,1,0:T(8,128)S(1)} collective-permute-done((f32[4,32,1024]{2,1,0:T(8,128)S(1)}, f32[4,32,1024]{2,1,0:T(8,128)S(1)}, u32[]{:S(2)}, u32[]{:S(2)}) %collective-permute-start.19) | collective-permute-done | bytes 524320 | tf_op jit(solution)/shard_map/ppermute | solution.py:25
  120.9 1.0 collective-permute-done.20
  121.9 14.0 %collective-permute-done.21 = f32[4,32,1024]{2,1,0:T(8,128)S(1)} collective-permute-done((f32[4,32,1024]{2,1,0:T(8,128)S(1)}, f32[4,32,1024]{2,1,0:T(8,128)S(1)}, u32[]{:S(2)}, u32[]{:S(2)}) %collective-permute-start.21) | collective-permute-done | bytes 524320 | tf_op jit(solution)/shard_map/ppermute | solution.py:25
  135.9 1.3 collective-permute-start.22
  137.1 1.3 collective-permute-start.23
  138.4 1.5 collective-permute-start.24
  140.0 1.3 collective-permute-start.25
  141.7 1.3 collective-permute-done.22
  143.0 8.7 %collective-permute-done.23 = f32[4,1024]{1,0:T(4,128)S(1)} collective-permute-done((f32[4,1024]{1,0:T(4,128)S(1)}, f32[4,1024]{1,0:T(4,128)S(1)}, u32[]{:S(2)}, u32[]{:S(2)}) %collective-permute-start.23) | collective-permute-done | bytes 16416 | tf_op jit(solution)/shard_map/ppermute | solution.py:142
  151.8 0.9 collective-permute-done.24
  152.7 1.0 collective-permute-done.25
  154.4 3.3 %all-to-all-start.1 = ((f32[8,4,4,128]{3,1,2,0:T(4,128)}), f32[8,4,4,128]{3,1,2,0:T(4,128)S(1)}, u32[]{:S(2)}, u32[]{:S(2)}) async-start(f32[8,4,4,128]{3,1,2,0:T(4,128)} %maximum_bitcast_fusion), calls=%async_computation.1 | async-start | bytes 131072 | tf_op jit(solution)/shard_map/all_to_all | solution.py:146
  157.8 1.1 bitcast_dynamic-update-slice_fusion
  158.8 6.1 %all-to-all-done.1 = f32[8,4,4,128]{3,1,2,0:T(4,128)S(1)} async-done(((f32[8,4,4,128]{3,1,2,0:T(4,128)}), f32[8,4,4,128]{3,1,2,0:T(4,128)S(1)}, u32[]{:S(2)}, u32[]{:S(2)}) %all-to-all-start.1) | async-done | bytes 65568 | tf_op jit(solution)/shard_map/all_to_all | solution.py:146
  165.0 0.7 fusion.10
  165.7 10.4 %all_to_all.16 = f32[8,4,1024]{2,1,0:T(4,128)S(1)} all-to-all(f32[8,4,1024]{2,1,0:T(4,128)S(1)} %fusion.10), channel_id=1, replica_groups={{0,32,64,96,128,160,192,224},{8,40,72,104,136,168,200,232},{16,48,80,11..., dimensions={0} | all-to-all | bytes 262144 | tf_op jit(solution)/shard_map/all_to_all | solution.py:48
  176.2 0.7 collective-permute-start.26
  176.9 0.7 collective-permute-start.27
  177.6 3.3 %select_subtract_fusion = (f32[4,1024]{1,0:T(4,128)S(1)}, f32[4,1024]{1,0:T(4,128)S(1)}) fusion(f32[4,1024]{1,0:T(4,128)S(1)} %sub.54, pred[]{:T(512)S(6)} %eq.82, f32[1024,1024]{1,0:T(8,128)} %all-gather.5.cloned.1.call-done, f32[4,1024]{1,0:T(4,128)S(1)} %collective-permute-done.26, f32[4,1024]{1,0:T(4,128)S(1)} %collective-permute-done.27, pred[]{:T(512)S(6)} %eq.86), kind=kOutput, calls=%fused_computation.43 | convolution fusion | flops 25182208 | bytes 4276226 | tf_op jit(solution)/shard_map/dot_general | solution.py:13
  180.9 1.3 collective-permute-start.28
  182.2 0.7 collective-permute-start.29
  182.9 1.6 collective-permute-start.30
  184.5 4.0 %collective-permute-done.28 = f32[4,1024]{1,0:T(4,128)S(1)} collective-permute-done((f32[4,1024]{1,0:T(4,128)S(1)}, f32[4,1024]{1,0:T(4,128)S(1)}, u32[]{:S(2)}, u32[]{:S(2)}) %collective-permute-start.28) | collective-permute-done | bytes 16416 | tf_op jit(solution)/shard_map/ppermute | solution.py:116
  188.5 3.3 %fusion.12 = f32[4,1024]{1,0:T(4,128)S(1)} fusion(f32[1024,1024]{1,0:T(8,128)} %all-gather.5.cloned.1.call-done, f32[4,1024]{1,0:T(4,128)S(1)} %collective-permute-done.28, f32[4,1024]{1,0:T(4,128)S(1)} %collective-permute-done.29), kind=kOutput, calls=%fused_computation.41 | convolution fusion | flops 25169920 | bytes 4243456 | tf_op jit(solution)/shard_map/dot_general | solution.py:13
  191.8 1.3 collective-permute-start.31
  193.1 0.7 collective-permute-start.33
  193.8 0.7 collective-permute-start.32
  194.5 1.4 fusion.28
  (68 shorter events, 5.2 us)
Async XLA Ops:
  6.5 1.2 copy-start
  6.5 93.1 %all-gather.3.cloned.1.call-start = ((), (), s32[]{:S(2)}) async-start(), calls=%async_computation.3 | async-start | bytes 4718592 | tf_op jit(solution)/shard_map/all_gather | solution.py:82
  7.8 24.8 %copy-start.6 = (s32[1024]{0:T(1024)S(1)}, s32[1024]{0:T(1024)}, u32[]{:S(2)}) copy-start(s32[1024]{0:T(1024)} %param.9) | copy-start | bytes 12292
  7.8 24.8 %copy-start.7 = (f32[16,1536]{1,0:T(8,128)S(1)}, f32[16,1536]{1,0:T(8,128)}, u32[]{:S(2)}) copy-start(f32[16,1536]{1,0:T(8,128)} %param.8) | copy-start | bytes 294916
  13.5 5.3 %collective-permute-start = (f32[32,1024]{1,0:T(8,128)S(1)}, f32[32,1024]{1,0:T(8,128)S(1)}, u32[]{:S(2)}, u32[]{:S(2)}) collective-permute-start(f32[32,1024]{1,0:T(8,128)S(1)} %get-tuple-element.50), channel_id=1, source_target_pairs={{5,7},{4,3},{0,6},{13,15},{12,11},{8,14},{21,23},{20,19},{16,22},{... | collective-permute-start | bytes 393224 | tf_op jit(solution)/shard_map/ppermute | solution.py:74
  14.2 6.5 %collective-permute-start.1 = (f32[32,1024]{1,0:T(8,128)S(1)}, f32[32,1024]{1,0:T(8,128)S(1)}, u32[]{:S(2)}, u32[]{:S(2)}) collective-permute-start(f32[32,1024]{1,0:T(8,128)S(1)} %get-tuple-element.49), channel_id=1, source_target_pairs={{4,2},{1,3},{0,7},{12,10},{9,11},{8,15},{20,18},{17,19},{16,23},{2... | collective-permute-start | bytes 393224 | tf_op jit(solution)/shard_map/ppermute | solution.py:75
  21.4 6.1 %collective-permute-start.10 = (f32[32,1024]{1,0:T(8,128)S(1)}, f32[32,1024]{1,0:T(8,128)S(1)}, u32[]{:S(2)}, u32[]{:S(2)}) collective-permute-start(f32[32,1024]{1,0:T(8,128)S(1)} %get-tuple-element.47), channel_id=1, source_target_pairs={{8,0},{16,8},{24,16},{0,24},{40,32},{48,40},{56,48},{32,56},{72,64... | collective-permute-start | bytes 393224 | tf_op jit(solution)/shard_map/ppermute | solution.py:25
  24.1 5.4 %collective-permute-start.11 = (f32[32,1024]{1,0:T(8,128)S(1)}, f32[32,1024]{1,0:T(8,128)S(1)}, u32[]{:S(2)}, u32[]{:S(2)}) collective-permute-start(f32[32,1024]{1,0:T(8,128)S(1)} %get-tuple-element.47), channel_id=1, source_target_pairs={{16,0},{24,8},{0,16},{8,24},{48,32},{56,40},{32,48},{40,56},{80,64... | collective-permute-start | bytes 393224 | tf_op jit(solution)/shard_map/ppermute | solution.py:25
  24.5 6.4 %collective-permute-start.12 = (f32[32,1024]{1,0:T(8,128)S(1)}, f32[32,1024]{1,0:T(8,128)S(1)}, u32[]{:S(2)}, u32[]{:S(2)}) collective-permute-start(f32[32,1024]{1,0:T(8,128)S(1)} %get-tuple-element.47), channel_id=1, source_target_pairs={{24,0},{0,8},{8,16},{16,24},{56,32},{32,40},{40,48},{48,56},{88,64... | collective-permute-start | bytes 393224 | tf_op jit(solution)/shard_map/ppermute | solution.py:25
  31.8 145.7 %all-gather.5.cloned.1.call-start = ((), (), s32[]{:S(2)}) async-start(), calls=%async_computation.4 | async-start | bytes 4718592 | tf_op jit(solution)/shard_map/all_gather | solution.py:82
  53.8 6.2 %collective-permute-start.2 = (f32[32,1024]{1,0:T(8,128)}, f32[32,1024]{1,0:T(8,128)}, u32[]{:S(2)}, u32[]{:S(2)}) collective-permute-start(f32[32,1024]{1,0:T(8,128)} %get-tuple-element.35), channel_id=1, source_target_pairs={{8,0},{16,8},{24,16},{0,24},{40,32},{48,40},{56,48},{32,56},{72,64... | collective-permute-start | bytes 393224 | tf_op jit(solution)/shard_map/ppermute | solution.py:25
  54.1 6.4 %collective-permute-start.3 = (f32[32,1024]{1,0:T(8,128)}, f32[32,1024]{1,0:T(8,128)}, u32[]{:S(2)}, u32[]{:S(2)}) collective-permute-start(f32[32,1024]{1,0:T(8,128)} %get-tuple-element.35), channel_id=1, source_target_pairs={{16,0},{24,8},{0,16},{8,24},{48,32},{56,40},{32,48},{40,56},{80,64... | collective-permute-start | bytes 393224 | tf_op jit(solution)/shard_map/ppermute | solution.py:25
  54.5 9.7 %collective-permute-start.4 = (f32[32,1024]{1,0:T(8,128)}, f32[32,1024]{1,0:T(8,128)}, u32[]{:S(2)}, u32[]{:S(2)}) collective-permute-start(f32[32,1024]{1,0:T(8,128)} %get-tuple-element.35), channel_id=1, source_target_pairs={{24,0},{0,8},{8,16},{16,24},{56,32},{32,40},{40,48},{48,56},{88,64... | collective-permute-start | bytes 393224 | tf_op jit(solution)/shard_map/ppermute | solution.py:25
  60.0 34.9 %copy-start.5 = (f32[4,1024]{1,0:T(4,128)S(1)}, f32[4,1024]{1,0:T(4,128)}, u32[]{:S(2)}) copy-start(f32[4,1024]{1,0:T(4,128)} %param.13) | copy-start | bytes 49156
  66.3 42.9 %copy-start.2 = (f32[4,32,1024]{2,1,0:T(8,128)}, f32[4,32,1024]{2,1,0:T(8,128)S(1)}, u32[]{:S(2)}) copy-start(f32[4,32,1024]{2,1,0:T(8,128)S(1)} %get-tuple-element.38) | copy-start | bytes 1572868
  66.6 4.7 %collective-permute-start.5 = (f32[8,4,1024]{2,1,0:T(4,128)S(1)}, f32[8,4,1024]{2,1,0:T(4,128)S(1)}, u32[]{:S(2)}, u32[]{:S(2)}) collective-permute-start(f32[8,4,1024]{2,1,0:T(4,128)S(1)} %get-tuple-element.51), channel_id=1, source_target_pairs={{8,0},{16,8},{24,16},{0,24},{40,32},{48,40},{56,48},{32,56},{72,64... | collective-permute-start | bytes 393224 | tf_op jit(solution)/shard_map/ppermute | solution.py:57
  66.7 5.4 %collective-permute-start.6 = (f32[8,4,1024]{2,1,0:T(4,128)S(1)}, f32[8,4,1024]{2,1,0:T(4,128)S(1)}, u32[]{:S(2)}, u32[]{:S(2)}) collective-permute-start(f32[8,4,1024]{2,1,0:T(4,128)S(1)} %get-tuple-element.53), channel_id=1, source_target_pairs={{16,0},{24,8},{0,16},{8,24},{48,32},{56,40},{32,48},{40,56},{80,64... | collective-permute-start | bytes 393224 | tf_op jit(solution)/shard_map/ppermute | solution.py:57
  67.0 9.4 %collective-permute-start.7 = (f32[8,4,1024]{2,1,0:T(4,128)S(1)}, f32[8,4,1024]{2,1,0:T(4,128)S(1)}, u32[]{:S(2)}, u32[]{:S(2)}) collective-permute-start(f32[8,4,1024]{2,1,0:T(4,128)S(1)} %get-tuple-element.52), channel_id=1, source_target_pairs={{24,0},{0,8},{8,16},{16,24},{56,32},{32,40},{40,48},{48,56},{88,64... | collective-permute-start | bytes 393224 | tf_op jit(solution)/shard_map/ppermute | solution.py:57
  98.2 1.3 collective-permute-start.8
  98.9 0.7 collective-permute-start.9
  102.9 2.0 collective-permute-start.13
  103.6 1.4 collective-permute-start.14
  104.3 4.0 %collective-permute-start.15 = (f32[4,1024]{1,0:T(4,128)S(1)}, f32[4,1024]{1,0:T(4,128)S(1)}, u32[]{:S(2)}, u32[]{:S(2)}) collective-permute-start(f32[4,1024]{1,0:T(4,128)S(1)} %get-tuple-element.63), channel_id=1, source_target_pairs={{7,5},{15,13},{23,21},{31,29},{39,37},{47,45},{55,53},{63,61},{71,... | collective-permute-start | bytes 49160 | tf_op jit(solution)/shard_map/ppermute | solution.py:116
  108.3 3.0 %collective-permute-start.16 = (f32[4,1024]{1,0:T(4,128)S(1)}, f32[4,1024]{1,0:T(4,128)S(1)}, u32[]{:S(2)}, u32[]{:S(2)}) collective-permute-start(f32[4,1024]{1,0:T(4,128)S(1)} %subtract_subtract_fusion.1), channel_id=1, source_target_pairs={{5,4},{13,12},{21,20},{29,28},{37,36},{45,44},{53,52},{61,60},{69,... | collective-permute-start | bytes 49160 | tf_op jit(solution)/shard_map/ppermute | solution.py:116
  109.0 11.9 %collective-permute-start.19 = (f32[4,32,1024]{2,1,0:T(8,128)S(1)}, f32[4,32,1024]{2,1,0:T(8,128)S(1)}, u32[]{:S(2)}, u32[]{:S(2)}) collective-permute-start(f32[4,32,1024]{2,1,0:T(8,128)S(1)} %get-tuple-element.38), channel_id=1, source_target_pairs={{8,0},{16,8},{24,16},{0,24},{40,32},{48,40},{56,48},{32,56},{72,64... | collective-permute-start | bytes 1572872 | tf_op jit(solution)/shard_map/ppermute | solution.py:25
  109.1 12.8 %collective-permute-start.20 = (f32[4,32,1024]{2,1,0:T(8,128)S(1)}, f32[4,32,1024]{2,1,0:T(8,128)S(1)}, u32[]{:S(2)}, u32[]{:S(2)}) collective-permute-start(f32[4,32,1024]{2,1,0:T(8,128)S(1)} %get-tuple-element.38), channel_id=1, source_target_pairs={{16,0},{24,8},{0,16},{8,24},{48,32},{56,40},{32,48},{40,56},{80,64... | collective-permute-start | bytes 1572872 | tf_op jit(solution)/shard_map/ppermute | solution.py:25
  109.2 26.7 %collective-permute-start.21 = (f32[4,32,1024]{2,1,0:T(8,128)S(1)}, f32[4,32,1024]{2,1,0:T(8,128)S(1)}, u32[]{:S(2)}, u32[]{:S(2)}) collective-permute-start(f32[4,32,1024]{2,1,0:T(8,128)S(1)} %get-tuple-element.38), channel_id=1, source_target_pairs={{24,0},{0,8},{8,16},{16,24},{56,32},{32,40},{40,48},{48,56},{88,64... | collective-permute-start | bytes 1572872 | tf_op jit(solution)/shard_map/ppermute | solution.py:25
  110.5 31.0 %copy-start.3 = (f32[4,32,1024]{2,1,0:T(8,128)S(1)}, f32[4,32,1024]{2,1,0:T(8,128)}, u32[]{:S(2)}) copy-start(f32[4,32,1024]{2,1,0:T(8,128)} %copy-done.2) | copy-start | bytes 1572868
  110.5 4.8 %collective-permute-start.18 = (f32[4,1024]{1,0:T(4,128)S(1)}, f32[4,1024]{1,0:T(4,128)S(1)}, u32[]{:S(2)}, u32[]{:S(2)}) collective-permute-start(f32[4,1024]{1,0:T(4,128)S(1)} %get-tuple-element.63), channel_id=1, source_target_pairs={{3,4},{11,12},{19,20},{27,28},{35,36},{43,44},{51,52},{59,60},{67,... | collective-permute-start | bytes 49160 | tf_op jit(solution)/shard_map/ppermute | solution.py:116
  111.3 4.0 %collective-permute-start.17 = (f32[4,1024]{1,0:T(4,128)S(1)}, f32[4,1024]{1,0:T(4,128)S(1)}, u32[]{:S(2)}, u32[]{:S(2)}) collective-permute-start(f32[4,1024]{1,0:T(4,128)S(1)} %fusion.17), channel_id=1, source_target_pairs={{2,4},{10,12},{18,20},{26,28},{34,36},{42,44},{50,52},{58,60},{66,... | collective-permute-start | bytes 49160 | tf_op jit(solution)/shard_map/ppermute | solution.py:116
  135.9 5.9 %copy-start.4 = (f32[4,32,1024]{2,1,0:T(8,128)}, f32[4,32,1024]{2,1,0:T(8,128)S(1)}, u32[]{:S(2)}) copy-start(f32[4,32,1024]{2,1,0:T(8,128)S(1)} %collective-permute-done.21) | copy-start | bytes 1572868
  135.9 7.2 %collective-permute-start.22 = (f32[4,1024]{1,0:T(4,128)S(1)}, f32[4,1024]{1,0:T(4,128)S(1)}, u32[]{:S(2)}, u32[]{:S(2)}) collective-permute-start(f32[4,1024]{1,0:T(4,128)S(1)} %add_subtract_fusion.1), channel_id=1, source_target_pairs={{4,0},{5,1},{6,2},{7,3},{12,8},{13,9},{14,10},{15,11},{20,16},{21,... | collective-permute-start | bytes 49160 | tf_op jit(solution)/shard_map/ppermute | solution.py:142
  137.1 14.6 %collective-permute-start.23 = (f32[4,1024]{1,0:T(4,128)S(1)}, f32[4,1024]{1,0:T(4,128)S(1)}, u32[]{:S(2)}, u32[]{:S(2)}) collective-permute-start(f32[4,1024]{1,0:T(4,128)S(1)} %add_subtract_fusion.1), channel_id=1, source_target_pairs={{5,0},{6,1},{7,2},{4,3},{13,8},{14,9},{15,10},{12,11},{21,16},{22,... | collective-permute-start | bytes 49160 | tf_op jit(solution)/shard_map/ppermute | solution.py:142
  138.4 14.3 %collective-permute-start.24 = (f32[4,1024]{1,0:T(4,128)S(1)}, f32[4,1024]{1,0:T(4,128)S(1)}, u32[]{:S(2)}, u32[]{:S(2)}) collective-permute-start(f32[4,1024]{1,0:T(4,128)S(1)} %add_subtract_fusion.1), channel_id=1, source_target_pairs={{6,0},{7,1},{4,2},{5,3},{14,8},{15,9},{12,10},{13,11},{22,16},{23,... | collective-permute-start | bytes 49160 | tf_op jit(solution)/shard_map/ppermute | solution.py:142
  140.0 13.8 %collective-permute-start.25 = (f32[4,1024]{1,0:T(4,128)S(1)}, f32[4,1024]{1,0:T(4,128)S(1)}, u32[]{:S(2)}, u32[]{:S(2)}) collective-permute-start(f32[4,1024]{1,0:T(4,128)S(1)} %add_subtract_fusion.1), channel_id=1, source_target_pairs={{7,0},{4,1},{5,2},{6,3},{15,8},{12,9},{13,10},{14,11},{23,16},{20,... | collective-permute-start | bytes 49160 | tf_op jit(solution)/shard_map/ppermute | solution.py:142
  154.4 10.6 %all-to-all-start.1 = ((f32[8,4,4,128]{3,1,2,0:T(4,128)}), f32[8,4,4,128]{3,1,2,0:T(4,128)S(1)}, u32[]{:S(2)}, u32[]{:S(2)}) async-start(f32[8,4,4,128]{3,1,2,0:T(4,128)} %maximum_bitcast_fusion), calls=%async_computation.1 | async-start | bytes 131072 | tf_op jit(solution)/shard_map/all_to_all | solution.py:146
  176.2 1.4 collective-permute-start.26
  176.9 0.7 collective-permute-start.27
  180.9 7.6 %collective-permute-start.28 = (f32[4,1024]{1,0:T(4,128)S(1)}, f32[4,1024]{1,0:T(4,128)S(1)}, u32[]{:S(2)}, u32[]{:S(2)}) collective-permute-start(f32[4,1024]{1,0:T(4,128)S(1)} %get-tuple-element.64), channel_id=1, source_target_pairs={{2,1},{10,9},{18,17},{26,25},{34,33},{42,41},{50,49},{58,57},{66,6... | collective-permute-start | bytes 49160 | tf_op jit(solution)/shard_map/ppermute | solution.py:116
  182.2 6.3 %collective-permute-start.29 = (f32[4,1024]{1,0:T(4,128)S(1)}, f32[4,1024]{1,0:T(4,128)S(1)}, u32[]{:S(2)}, u32[]{:S(2)}) collective-permute-start(f32[4,1024]{1,0:T(4,128)S(1)} %get-tuple-element.64), channel_id=1, source_target_pairs={{2,6},{10,14},{18,22},{26,30},{34,38},{42,46},{50,54},{58,62},{66,... | collective-permute-start | bytes 49160 | tf_op jit(solution)/shard_map/ppermute | solution.py:116
  182.9 11.6 %copy-start.1 = (f32[1024,1024]{1,0:T(8,128)S(1)}, f32[1024,1024]{1,0:T(8,128)}, u32[]{:S(2)}) copy-start(f32[1024,1024]{1,0:T(8,128)} %all-gather.5.cloned.1.call-done) | copy-start | bytes 12582916
  182.9 8.9 %collective-permute-start.30 = (f32[4,1024]{1,0:T(4,128)S(1)}, f32[4,1024]{1,0:T(4,128)S(1)}, u32[]{:S(2)}, u32[]{:S(2)}) collective-permute-start(f32[4,1024]{1,0:T(4,128)S(1)} %get-tuple-element.65), channel_id=1, source_target_pairs={{3,1},{11,9},{19,17},{27,25},{35,33},{43,41},{51,49},{59,57},{67,6... | collective-permute-start | bytes 49160 | tf_op jit(solution)/shard_map/ppermute | solution.py:116
  191.8 2.6 %collective-permute-start.31 = (f32[4,1024]{1,0:T(4,128)S(1)}, f32[4,1024]{1,0:T(4,128)S(1)}, u32[]{:S(2)}, u32[]{:S(2)}) collective-permute-start(f32[4,1024]{1,0:T(4,128)S(1)} %subtract_subtract_fusion), channel_id=1, source_target_pairs={{1,0},{9,8},{17,16},{25,24},{33,32},{41,40},{49,48},{57,56},{65,64... | collective-permute-start | bytes 49160 | tf_op jit(solution)/shard_map/ppermute | solution.py:116
  193.1 2.7 %collective-permute-start.33 = (f32[4,1024]{1,0:T(4,128)S(1)}, f32[4,1024]{1,0:T(4,128)S(1)}, u32[]{:S(2)}, u32[]{:S(2)}) collective-permute-start(f32[4,1024]{1,0:T(4,128)S(1)} %get-tuple-element.65), channel_id=1, source_target_pairs={{7,0},{15,8},{23,16},{31,24},{39,32},{47,40},{55,48},{63,56},{71,6... | collective-permute-start | bytes 49160 | tf_op jit(solution)/shard_map/ppermute | solution.py:116
  193.8 2.1 %collective-permute-start.32 = (f32[4,1024]{1,0:T(4,128)S(1)}, f32[4,1024]{1,0:T(4,128)S(1)}, u32[]{:S(2)}, u32[]{:S(2)}) collective-permute-start(f32[4,1024]{1,0:T(4,128)S(1)} %fusion.12), channel_id=1, source_target_pairs={{6,0},{14,8},{22,16},{30,24},{38,32},{46,40},{54,48},{62,56},{70,6... | collective-permute-start | bytes 49160 | tf_op jit(solution)/shard_map/ppermute | solution.py:116
Sparse Core Ops, SparseCore 0:
  32.0 63.2 all-gather.2
  97.0 53.5 all-gather.4
